TPU v7x, 32 devices: a whole 2x2x4 slice. The times are simulated.
32 devices in a mesh: shard: 2 (over x), ctx: 4 (over z), tp: 4 (over y, core).
Axes of the slice: x: 2, y: 2, z: 4, core: 2. Of those that a mesh axis runs over, the one named last changes fastest.
Arguments:
- frames: bfloat16 [2, 2, 2048, 1280], P(None, 'shard', 'ctx'), may hold values from -6 to 6
- lengths: int32 [2, 2], P(None, 'shard'), may hold values from 0 to 2048, as said below
- first_gain: bfloat16 [1280], replicated, may hold values from 0.25 to 1.75
- first_bias: bfloat16 [1280], replicated, may hold values from -3 to 3
- query_weight: bfloat16 [1280, 1280], P('shard', 'tp'), may hold values from -0.15625 to 0.15625
- query_bias: bfloat16 [1280], P('tp'), may hold values from -3 to 3
- key_weight: bfloat16 [1280, 1280], P('shard', 'tp'), may hold values from -0.15625 to 0.15625
- value_weight: bfloat16 [1280, 1280], P('shard', 'tp'), may hold values from -0.15625 to 0.15625
- value_bias: bfloat16 [1280], P('tp'), may hold values from -0.088378906 to 0.088378906
- output_weight: bfloat16 [1280, 1280], P('shard', 'tp'), may hold values from -4 to 4
- output_bias: bfloat16 [1280], replicated, may hold values from -3 to 3
- second_gain: bfloat16 [1280], replicated, may hold values from 0.25 to 1.75
- second_bias: bfloat16 [1280], replicated, may hold values from -3 to 3
- inner_weight: bfloat16 [1280, 5120], P('shard', 'tp'), may hold values from -0.15625 to 0.15625
- inner_bias: bfloat16 [5120], P('tp'), may hold values from -3 to 3
- outer_weight: bfloat16 [1280, 5120], P('shard', 'tp'), may hold values from -0.15625 to 0.15625
- outer_bias: bfloat16 [1280], replicated, may hold values from -3 to 3
- cotangent: bfloat16 [2, 2, 2048, 1280], P(None, 'shard', 'ctx'), may hold values from -6 to 6
Outputs:
- result: bfloat16 [2, 2, 2048, 1280], P(None, 'shard', 'ctx')
- frames_grad: bfloat16 [2, 2, 2048, 1280], P(None, 'shard', 'ctx')
- first_gain_grad: float32 [1280], replicated
- first_bias_grad: float32 [1280], replicated
- query_weight_grad: float32 [1280, 1280], P('shard', 'tp')
- query_bias_grad: float32 [1280], P('tp')
- key_weight_grad: float32 [1280, 1280], P('shard', 'tp')
- value_weight_grad: float32 [1280, 1280], P('shard', 'tp')
- value_bias_grad: float32 [1280], P('tp')
- output_weight_grad: float32 [1280, 1280], P('shard', 'tp')
- output_bias_grad: float32 [1280], replicated
- second_gain_grad: float32 [1280], replicated
- second_bias_grad: float32 [1280], replicated
- inner_weight_grad: float32 [1280, 5120], P('shard', 'tp')
- inner_bias_grad: float32 [5120], P('tp')
- outer_weight_grad: float32 [1280, 5120], P('shard', 'tp')
- outer_bias_grad: float32 [1280], replicated
Inputs may be any that keep to these rules, and one draw needn't show every extreme that they name: Slot lengths count a clip's first frames; 0 marks an empty slot; in every draw some slot is empty and some slot is full.
All inputs are finite; a program needn't handle non-finite values.
Results may differ from a plain program's by a relative error of at most 0.025.
Values may be sent and summed in bfloat16 or wider, within the bound.
No kernel may reach another device: no remote copies, remote signals or barrier semaphores. Data moves between devices by JAX's collectives and lax.ppermute only.
A program may use at most 192 MiB of HBM per device.

v0:
```python
import functools
import math
import types

import jax
import jax.numpy as jnp
from jax import lax
from jax.experimental import pallas as pl
from jax.experimental.pallas import tpu as pltpu
from jax.sharding import PartitionSpec as P


HD = 80
EXT = 96
EPS = 1e-05
BF = jnp.bfloat16
F32 = jnp.float32
SCALE = 1.0 / math.sqrt(HD)
SCALE2 = SCALE * math.log2(math.e)
SLOTS = (0, 2, 1, 3)
NT = (((1,), (1,)), ((), ()))
TN = (((0,), (0,)), ((), ()))


def sds(shape, kind):
    return jax.ShapeDtypeStruct(shape, kind)


def dot(left, right):
    return jnp.dot(left, right, preferred_element_type=F32)


def dot_nt(left, right):
    return lax.dot_general(left, right, NT, preferred_element_type=F32)


def dot_tn(left, right):
    return lax.dot_general(left, right, TN, preferred_element_type=F32)


def tie(value, *others):
    return lax.optimization_barrier((value,) + others)[0]


def normalize(values):
    center = values - jnp.mean(values, -1, keepdims=True)
    spread = jnp.mean(center * center, -1, keepdims=True)
    inverse = lax.rsqrt(spread + EPS)
    return center * inverse, inverse


def norm_back(unit, inverse, grad, gain):
    scaled = grad * gain
    first = jnp.mean(scaled, -1, keepdims=True)
    second = jnp.mean(scaled * unit, -1, keepdims=True)
    return inverse * (scaled - first - unit * second)


SMEM = pl.BlockSpec(memory_space=pltpu.SMEM)


def front_kernel(micro, ids, fa, fb, ca, cb, gain, bias, normed_o, low_o):
    half = fa.shape[-1]
    rows = fa.shape[-2]
    piece = pl.program_id(0)
    va = fa[0].astype(F32)
    vb = fb[0].astype(F32)
    count = 2 * half
    mean = (jnp.sum(va, -1, keepdims=True) + jnp.sum(vb, -1, keepdims=True)) / count
    va = va - mean
    vb = vb - mean
    spread = (jnp.sum(va * va, -1, keepdims=True) + jnp.sum(vb * vb, -1, keepdims=True)) / count
    inverse = lax.rsqrt(spread + EPS)
    normed_o[:, :half] = (va * inverse * gain[:, :half] + bias[:, :half]).astype(BF)
    normed_o[:, half:] = (vb * inverse * gain[:, half:] + bias[:, half:]).astype(BF)
    start = ids[6] * (rows * 4) + ids[piece] * rows
    valid = start + lax.broadcasted_iota(jnp.int32, (rows, 1), 0) < ids[8 + micro]
    low_o[:, :half] = jnp.where(valid, ca[0].astype(F32), 0.0).astype(BF)
    low_o[:, half:] = jnp.where(valid, cb[0].astype(F32), 0.0).astype(BF)


def front(micro, ids, frames, cotangent, gain, bias):
    rows, width = frames.shape[1:]
    quarter = rows // 4
    half = width // 2
    own = pl.BlockSpec((1, quarter, half), lambda p, ids: (micro, ids[p], ids[4]))
    other = pl.BlockSpec((1, quarter, half), lambda p, ids: (micro, ids[p], ids[5]))
    line = pl.BlockSpec((1, width), lambda p, ids: (0, 0))
    out = pl.BlockSpec((quarter, width), lambda p, ids: (p, 0))
    return pl.pallas_call(
        functools.partial(front_kernel, micro),
        out_shape=(sds((rows, width), BF), sds((rows, width), BF)),
        grid_spec=pltpu.PrefetchScalarGridSpec(
            num_scalar_prefetch=1,
            grid=(4,),
            in_specs=[own, other, own, other, line, line],
            out_specs=[out, out],
        ),
    )(ids, frames, frames, cotangent, cotangent, gain, bias)


def heads_out(ids, store, offset, outs):
    for slot in range(len(outs)):
        begin = pl.multiple_of((ids[6] ^ slot) * HD, 16)
        outs[slot][offset : offset + HD, :] = store[pl.ds(begin, HD), :]


def project_kernel(ids, normed, qa, qb, ka, kb, va, vb, q_bias, v_bias, o0, o1, o2, o3, store):
    half = qa.shape[0]
    left = normed[:, :half]
    right = normed[:, half:]
    outs = (o0, o1, o2, o3)
    for order, (first, second, shift) in enumerate(
        ((qa, qb, q_bias), (ka, kb, None), (va, vb, v_bias))
    ):
        value = dot(left, first[...]) + dot(right, second[...])
        if shift is not None:
            value = value + shift[...]
        store[...] = value.T.astype(BF)
        heads_out(ids, store, order * HD, outs)


def project(ids, normed, weights, q_bias, v_bias):
    rows = normed.shape[0]
    width = weights[0].shape[1]
    return pl.pallas_call(
        project_kernel,
        out_shape=tuple(sds((3 * HD, rows), BF) for _ in range(4)),
        in_specs=[SMEM] + [pl.BlockSpec()] * 9,
        scratch_shapes=[pltpu.VMEM((width, rows), BF)],
    )(ids, normed, *weights, q_bias, v_bias)


def attend_kernel(plan, x0, x1, x2, x3, mask, o0, o1, o2, o3, kept, total, qs, ks, vs):
    rows = x0.shape[1]
    tail = EXT - HD
    first = lax.broadcasted_iota(jnp.int32, (tail, rows), 0) == 0
    ones = jnp.where(first, 1.0, 0.0).astype(BF)
    for slot, ref in enumerate((x0, x1, x2, x3)):
        qs[slot, :HD, :] = ref[:HD, :]
        qs[slot, HD:, :] = ones
        vs[slot, :HD, :] = ref[2 * HD :, :]
        vs[slot, HD:, :] = ones
        shift = jnp.where(first, mask[slot], 0.0)
        whole = jnp.concatenate([ref[HD : 2 * HD, :].astype(F32), shift], 0)
        ks[slot] = whole.T.astype(BF)
    has = plan[0] > 0

    def query_step(i, carry):
        query = qs[i]

        def key_step(n, acc):
            j = plan[1 + n]
            score = dot(ks[j], query)
            expo = jnp.exp2(score * SCALE2).astype(BF)
            return acc + dot(vs[j], expo)

        acc = lax.fori_loop(0, plan[0], key_step, jnp.zeros((EXT, rows), F32))
        denom = jnp.where(has, acc[HD : HD + 1, :], 1.0)
        attended = acc[:HD, :] / denom
        kept[i] = attended
        total[i] = denom
        return carry

    lax.fori_loop(0, 4, query_step, 0)
    for slot, ref in enumerate((o0, o1, o2, o3)):
        ref[...] = kept[slot].astype(BF)


def attend(plan, slabs, mask):
    rows = slabs[0].shape[1]
    return pl.pallas_call(
        attend_kernel,
        out_shape=tuple(sds((HD, rows), BF) for _ in range(4))
        + (sds((4, HD, rows), F32), sds((4, 1, rows), F32)),
        in_specs=[SMEM] + [pl.BlockSpec()] * 5,
        scratch_shapes=[
            pltpu.VMEM((4, EXT, rows), BF),
            pltpu.VMEM((4, rows, EXT), BF),
            pltpu.VMEM((4, EXT, rows), BF),
        ],
    )(plan, *slabs, mask)


def attend_back_kernel(
    plan,
    x0,
    x1,
    x2,
    x3,
    g0,
    g1,
    g2,
    g3,
    kept,
    total,
    mask,
    o0,
    o1,
    o2,
    o3,
    qs,
    qt,
    ks,
    kt,
    vs,
    ss,
    st,
    deltas,
    gq,
    gk,
    gv,
):
    rows = x0.shape[1]
    tail = EXT - HD
    first = lax.broadcasted_iota(jnp.int32, (tail, rows), 0) == 0
    ones = jnp.where(first, 1.0, 0.0).astype(BF)
    blank = jnp.zeros((tail, rows), BF)
    blank_wide = jnp.zeros((tail, rows), F32)
    for slot, (ref, grad_ref) in enumerate(zip((x0, x1, x2, x3), (g0, g1, g2, g3))):
        qs[slot, :HD, :] = ref[:HD, :]
        qs[slot, HD:, :] = ones
        qt[slot] = jnp.concatenate([ref[:HD, :].astype(F32), blank_wide], 0).T.astype(BF)
        kt[slot] = ref[HD : 2 * HD, :]
        shift = jnp.where(first, mask[slot], 0.0)
        ks[slot] = jnp.concatenate([ref[HD : 2 * HD, :].astype(F32), shift], 0).T.astype(BF)
        vs[slot] = jnp.concatenate([ref[2 * HD :, :].astype(F32), blank_wide], 0).T.astype(BF)
        grad = grad_ref[...].astype(F32)
        recip = 1.0 / total[slot]
        deltas[slot] = jnp.sum(grad * kept[slot], 0, keepdims=True) * recip
        scaled = (grad * recip).astype(BF)
        ss[slot, :HD, :] = scaled
        ss[slot, HD:, :] = blank
        st[slot] = jnp.concatenate([scaled.astype(F32), blank_wide], 0).T.astype(BF)
    gq[...] = jnp.zeros_like(gq)
    gk[...] = jnp.zeros_like(gk)
    gv[...] = jnp.zeros_like(gv)

    def query_step(m, carry):
        i = plan[1 + m]

        def key_step(n, acc):
            j = plan[1 + n]
            score = dot(ks[j], qs[i])
            expo = jnp.exp2(score * SCALE2)
            through = dot(vs[j], ss[i])
            raw = (expo * (through - deltas[i])).astype(BF)
            gv[j] += dot(expo.astype(BF), st[i])
            gk[j] += dot(raw, qt[i])
            return acc + dot(kt[j], raw)

        gq[i] = lax.fori_loop(0, plan[0], key_step, jnp.zeros((HD, rows), F32))
        return carry

    lax.fori_loop(0, plan[0], query_step, 0)
    for slot, ref in enumerate((o0, o1, o2, o3)):
        ref[:HD, :] = (gq[slot] * SCALE).astype(BF)
        ref[HD : 2 * HD, :] = (gk[slot] * SCALE).T[:HD, :].astype(BF)
        ref[2 * HD :, :] = gv[slot].T[:HD, :].astype(BF)


def attend_back(plan, slabs, grads, kept, total, mask):
    rows = slabs[0].shape[1]
    return pl.pallas_call(
        attend_back_kernel,
        out_shape=tuple(sds((3 * HD, rows), BF) for _ in range(4)),
        in_specs=[SMEM] + [pl.BlockSpec()] * 11,
        scratch_shapes=[
            pltpu.VMEM((4, EXT, rows), BF),
            pltpu.VMEM((4, rows, EXT), BF),
            pltpu.VMEM((4, rows, EXT), BF),
            pltpu.VMEM((4, HD, rows), BF),
            pltpu.VMEM((4, rows, EXT), BF),
            pltpu.VMEM((4, EXT, rows), BF),
            pltpu.VMEM((4, rows, EXT), BF),
            pltpu.VMEM((4, 1, rows), F32),
            pltpu.VMEM((4, HD, rows), F32),
            pltpu.VMEM((4, rows, EXT), F32),
            pltpu.VMEM((4, rows, EXT), F32),
        ],
    )(plan, *slabs, *grads, kept, total, mask)


def split_out(left, right, half, keep_a, keep_b, send_a, send_b):
    quarter = keep_a.shape[0]
    for value, lanes in ((left, slice(0, half)), (right, slice(half, 2 * half))):
        send_b[:, lanes] = value[3 * quarter :].astype(BF)
        send_a[:, lanes] = value[2 * quarter : 3 * quarter].astype(BF)
        keep_b[:, lanes] = value[quarter : 2 * quarter]
        keep_a[:, lanes] = value[:quarter]


def parts_shape(quarter, width):
    return (
        sds((quarter, width), F32),
        sds((quarter, width), F32),
        sds((quarter, width), BF),
        sds((quarter, width), BF),
    )


def output_kernel(ids, m0, m1, m2, m3, wa, wb, mixed_o, keep_a, keep_b, send_a, send_b, store):
    for slot, ref in enumerate((m0, m1, m2, m3)):
        begin = pl.multiple_of((ids[6] ^ slot) * HD, 16)
        store[pl.ds(begin, HD), :] = ref[...]
    mixed = store[...].astype(F32).T.astype(BF)
    mixed_o[...] = mixed
    half = wa.shape[0]
    split_out(
        dot_nt(mixed, wa[...]), dot_nt(mixed, wb[...]), half, keep_a, keep_b, send_a, send_b
    )


def output_part(ids, slabs, weights):
    rows = slabs[0].shape[1]
    half, width = weights[0].shape
    return pl.pallas_call(
        output_kernel,
        out_shape=(sds((rows, width), BF),) + parts_shape(rows // 4, 2 * half),
        in_specs=[SMEM] + [pl.BlockSpec()] * 6,
        scratch_shapes=[pltpu.VMEM((width, rows), BF)],
    )(ids, *slabs, *weights)


def middle_kernel(keep, first, second, frames, shift, gain, bias, middle_o, low_o):
    middle = (
        frames[...].astype(F32)
        + (keep[...] + first[...].astype(F32) + second[...].astype(F32))
        + shift[...]
    )
    middle_o[...] = middle
    unit, _ = normalize(middle)
    low_o[...] = (unit * gain[...] + bias[...]).astype(BF)


def middle_norm(keep, first, second, frames, shift, gain, bias):
    shape = keep.shape
    return pl.pallas_call(
        middle_kernel, out_shape=(sds(shape, F32), sds(shape, BF))
    )(keep, first, second, frames, shift, gain, bias)


def feed_kernel(
    n0,
    n1,
    n2,
    n3,
    low,
    ia,
    ib,
    oa,
    ob,
    shift,
    normed_o,
    active_o,
    inner_o,
    shift_o,
    fa,
    fb,
    fc,
    fd,
    ba,
    bb,
    bc,
    bd,
    acc_f,
    acc_b,
):
    step = pl.program_id(0)
    half = ia.shape[0]
    quarter = n0.shape[0]

    @pl.when(step == 0)
    def _():
        for slot, ref in enumerate((n0, n1, n2, n3)):
            normed_o[slot * quarter : (slot + 1) * quarter, :] = ref[...]
        acc_f[...] = jnp.zeros_like(acc_f)
        acc_b[...] = jnp.zeros_like(acc_b)

    inner = dot(normed_o[:, :half], ia[...]) + dot(normed_o[:, half:], ib[...]) + shift[...]
    chance = 0.5 * (1.0 + lax.erf(inner * math.sqrt(0.5)))
    active = (inner * chance).astype(BF)
    active_o[...] = active
    slope = chance + inner * jnp.exp(-0.5 * inner * inner) * (1.0 / math.sqrt(2.0 * math.pi))
    grad = (dot(low[:, :half], oa[...]) + dot(low[:, half:], ob[...])) * slope
    shift_o[...] = jnp.sum(grad, 0, keepdims=True)
    grad_low = grad.astype(BF)
    inner_o[...] = grad_low
    acc_b[:, :half] += dot_nt(grad_low, ia[...])
    acc_b[:, half:] += dot_nt(grad_low, ib[...])
    acc_f[:, :half] += dot_nt(active, oa[...])
    acc_f[:, half:] += dot_nt(active, ob[...])

    @pl.when(step == pl.num_programs(0) - 1)
    def _():
        split_out(acc_b[:, :half], acc_b[:, half:], half, ba, bb, bc, bd)
        split_out(acc_f[:, :half], acc_f[:, half:], half, fa, fb, fc, fd)


def feed(parts, low, inner, outer, shift):
    quarter, width = parts[0].shape
    rows = 4 * quarter
    half, hidden = inner[0].shape
    block = 256
    whole = lambda *shape: pl.BlockSpec(shape, lambda f: (0,) * len(shape))
    cols = lambda count: pl.BlockSpec((count, block), lambda f: (0, f))
    part = whole(quarter, width)
    return pl.pallas_call(
        feed_kernel,
        grid=(hidden // block,),
        out_shape=(
            sds((rows, width), BF),
            sds((rows, hidden), BF),
            sds((rows, hidden), BF),
            sds((1, hidden), F32),
        )
        + parts_shape(quarter, width)
        + parts_shape(quarter, width),
        in_specs=[part] * 4 + [whole(rows, width)] + [cols(half)] * 4 + [cols(1)],
        out_specs=(whole(rows, width), cols(rows), cols(rows), cols(1)) + (part,) * 8,
        scratch_shapes=[pltpu.VMEM((rows, width), F32), pltpu.VMEM((rows, width), F32)],
    )(*parts, low, *inner, *outer, shift)


def middle_back_kernel(
    keep, first, second, middle, final, gain, grad_o, low_o, gain_o, bias_o, shift_o
):
    grad = keep[...] + first[...].astype(F32) + second[...].astype(F32)
    unit, inverse = normalize(middle[...])
    gain_o[...] = jnp.sum(grad * unit, 0, keepdims=True)
    bias_o[...] = jnp.sum(grad, 0, keepdims=True)
    total = final[...].astype(F32) + norm_back(unit, inverse, grad, gain[...])
    grad_o[...] = total
    low_o[...] = total.astype(BF)
    shift_o[...] = jnp.sum(total, 0, keepdims=True)


def middle_back(keep, first, second, middle, final, gain):
    shape = keep.shape
    line = sds((1, shape[1]), F32)
    return pl.pallas_call(
        middle_back_kernel,
        out_shape=(sds(shape, F32), sds(shape, BF), line, line, line),
    )(keep, first, second, middle, final, gain)


def attended_kernel(ids, l0, l1, l2, l3, wa, wb, low_o, o0, o1, o2, o3, store):
    half = wa.shape[0]
    quarter = l0.shape[0]
    for slot, ref in enumerate((l0, l1, l2, l3)):
        low_o[slot * quarter : (slot + 1) * quarter, :] = ref[...]
    value = dot(low_o[:, :half], wa[...]) + dot(low_o[:, half:], wb[...])
    store[...] = value.T.astype(BF)
    heads_out(ids, store, 0, (o0, o1, o2, o3))


def attended_grad(ids, parts, weights):
    quarter, width = parts[0].shape
    rows = 4 * quarter
    group = weights[0].shape[1]
    return pl.pallas_call(
        attended_kernel,
        out_shape=(sds((rows, width), BF),) + tuple(sds((HD, rows), BF) for _ in range(4)),
        in_specs=[SMEM] + [pl.BlockSpec()] * 6,
        scratch_shapes=[pltpu.VMEM((group, rows), BF)],
    )(ids, *parts, *weights)


def project_back_kernel(
    ids,
    s0,
    s1,
    s2,
    s3,
    qa,
    qb,
    ka,
    kb,
    va,
    vb,
    gq,
    gk,
    gv,
    q_sum,
    v_sum,
    keep_a,
    keep_b,
    send_a,
    send_b,
    store,
):
    half = qa.shape[0]
    left = None
    right = None
    for order, (first, second, out, total) in enumerate(
        ((qa, qb, gq, q_sum), (ka, kb, gk, None), (va, vb, gv, v_sum))
    ):
        for slot, ref in enumerate((s0, s1, s2, s3)):
            begin = pl.multiple_of((ids[6] ^ slot) * HD, 16)
            store[pl.ds(begin, HD), :] = ref[order * HD : (order + 1) * HD, :]
        wide = store[...].astype(F32).T
        grad = wide.astype(BF)
        out[...] = grad
        if total is not None:
            total[...] = jnp.sum(wide, 0, keepdims=True)
        term_left = dot_nt(grad, first[...])
        term_right = dot_nt(grad, second[...])
        left = term_left if left is None else left + term_left
        right = term_right if right is None else right + term_right
    split_out(left, right, half, keep_a, keep_b, send_a, send_b)


def project_back(ids, slabs, weights):
    rows = slabs[0].shape[1]
    half, group = weights[0].shape
    return pl.pallas_call(
        project_back_kernel,
        out_shape=tuple(sds((rows, group), BF) for _ in range(3))
        + (sds((1, group), F32), sds((1, group), F32))
        + parts_shape(rows // 4, 2 * half),
        in_specs=[SMEM] + [pl.BlockSpec()] * 10,
        scratch_shapes=[pltpu.VMEM((group, rows), BF)],
    )(ids, *slabs, *weights)


def first_back_kernel(keep, first, second, frames, middle_grad, gain, out_o, gain_o, bias_o):
    grad = keep[...] + first[...].astype(F32) + second[...].astype(F32)
    unit, inverse = normalize(frames[...].astype(F32))
    gain_o[...] = jnp.sum(grad * unit, 0, keepdims=True)
    bias_o[...] = jnp.sum(grad, 0, keepdims=True)
    out_o[...] = (middle_grad[...] + norm_back(unit, inverse, grad, gain[...])).astype(BF)


def first_back(keep, first, second, frames, middle_grad, gain):
    shape = keep.shape
    line = sds((1, shape[1]), F32)
    return pl.pallas_call(
        first_back_kernel, out_shape=(sds(shape, BF), line, line)
    )(keep, first, second, frames, middle_grad, gain)


def gather_kernel(ids, *refs):
    out = refs[-1]
    micro = pl.program_id(0)
    piece = pl.program_id(1)
    half = out.shape[-1] // 2
    for m in range(len(refs) // 4):
        for p in range(4):

            @pl.when((micro == m) & (piece == p))
            def _(ref=refs[4 * m + p]):
                left = ref[:, :half]
                right = ref[:, half:]

                @pl.when(ids[4] == 0)
                def _():
                    out[0, 0, :, :half] = left
                    out[0, 0, :, half:] = right

                @pl.when(ids[4] != 0)
                def _():
                    out[0, 0, :, :half] = right
                    out[0, 0, :, half:] = left


def gather_rows(ids, parts):
    quarter, width = parts[0].shape
    micros = len(parts) // 4
    return pl.pallas_call(
        gather_kernel,
        out_shape=sds((micros, 1, 4 * quarter, width), BF),
        grid_spec=pltpu.PrefetchScalarGridSpec(
            num_scalar_prefetch=1,
            grid=(micros, 4),
            in_specs=[pl.BlockSpec((quarter, width), lambda m, p, ids: (0, 0))] * len(parts),
            out_specs=pl.BlockSpec((1, 1, quarter, width), lambda m, p, ids: (m, 0, ids[p], 0)),
        ),
    )(ids, *parts)


def per_device(
    sizes,
    frames,
    lengths,
    first_gain,
    first_bias,
    query_weight,
    query_bias,
    key_weight,
    value_weight,
    value_bias,
    output_weight,
    output_bias,
    second_gain,
    second_bias,
    inner_weight,
    inner_bias,
    outer_weight,
    outer_bias,
    cotangent,
):
    shard_count = sizes["shard"]
    ctx_count = sizes["ctx"]
    tp_count = sizes["tp"]
    assert ctx_count == 4 and tp_count == 4
    micros = frames.shape[0]
    rows = frames.shape[2]
    width = frames.shape[3]
    half = width // 2
    quarter = rows // 4
    paired = shard_count == 2
    tp_at = lax.axis_index("tp")
    ctx_at = lax.axis_index("ctx")
    shard_at = lax.axis_index("shard") if paired else jnp.int32(0)

    def core(value):
        return lax.ppermute(value, "tp", [(i, i ^ 1) for i in range(4)])

    def across(value):
        return lax.ppermute(value, "tp", [(i, i ^ 2) for i in range(4)])

    def blocks(value, slot):
        return lax.ppermute(value, "ctx", [(i, i ^ slot) for i in range(4)])

    def mate(value):
        return lax.ppermute(value, "shard", [(0, 1), (1, 0)])

    order = [tp_at ^ slot for slot in SLOTS]
    ids = jnp.stack(
        [jnp.int32(v) for v in order]
        + [shard_at, 1 - shard_at if paired else jnp.int32(1), ctx_at, tp_at]
        + [lengths[m, 0] for m in range(micros)]
    ).astype(jnp.int32)

    def turn(line):
        if not paired:
            return line
        return jnp.where(shard_at == 0, line, jnp.roll(line, half, -1))

    def line_of(vector):
        return turn(vector.astype(F32)[None, :])

    gain_one = line_of(first_gain)
    bias_one = line_of(first_bias)
    gain_two = line_of(second_gain)
    bias_two = line_of(second_bias)
    output_shift = line_of(output_bias)
    outer_shift = line_of(outer_bias)
    query_shift = query_bias.astype(F32)[None, :]
    value_shift = value_bias.astype(F32)[None, :]
    inner_shift = inner_bias.astype(F32)[None, :]

    held = {}

    def fetch(name, weight, after=None):
        if paired:
            sent = weight if after is None else tie(weight, after)
            held[name] = (weight, mate(sent))
        else:
            full = lax.all_gather(weight, "shard", axis=0, tiled=True)
            held[name] = (full[:half], full[half:])
        return held[name][1]

    got_q = fetch("q", query_weight)
    got_k = fetch("k", key_weight)
    got_v = fetch("v", value_weight)
    fetch("o", output_weight, got_v)
    fetch("f", outer_weight, got_v)
    fetch("i", inner_weight, got_v)
    qkv = held["q"] + held["k"] + held["v"]

    frames_in = frames[:, 0]
    cotangent_in = cotangent[:, 0]
    offsets = jnp.concatenate(
        [quarter * v + jnp.arange(quarter, dtype=jnp.int32) for v in order]
    )

    def cut_own(array, m):
        return turn(lax.dynamic_slice_in_dim(array[m], order[0] * quarter, quarter, 0))

    def reduce_rows(parts):
        keep_a, keep_b, send_a, send_b = parts
        near_b = core(send_b)
        near_a = core(send_a)
        far = across((keep_b + near_b.astype(F32)).astype(BF))
        return keep_a, near_a, far

    def spread_rows(own):
        far = across(own)
        near = core(own)
        return own, far, near, core(far)

    def exchange(slabs):
        return (slabs[0],) + tuple(blocks(slabs[s], s) for s in range(1, 4))

    state = [types.SimpleNamespace() for _ in range(micros)]
    for m in range(micros):
        s = state[m]
        length = lengths[m, 0]
        s.normed, s.low = front(m, ids, frames_in, cotangent_in, gain_one, bias_one)
        s.own = cut_own(frames_in, m)
        starts = jnp.stack([(ctx_at ^ slot) * rows for slot in range(4)])
        s.mask = jnp.where(
            starts[:, None, None] + offsets[None, None, :] < length, 0.0, -1e30
        ).astype(F32)
        live = (starts < length).astype(jnp.int32)
        places = jnp.cumsum(live) - live
        listed = jnp.sum(
            jnp.where(
                (live[None, :] == 1) & (places[None, :] == jnp.arange(4)[:, None]),
                jnp.arange(4)[None, :],
                0,
            ),
            -1,
        )
        s.plan = jnp.concatenate([jnp.sum(live)[None], listed]).astype(jnp.int32)
    for m in range(micros):
        s = state[m]
        slabs = project(ids, s.normed, qkv, query_shift, value_shift)
        s.slabs = exchange(slabs)
    for m in range(micros):
        s = state[m]
        found = attend(s.plan, s.slabs, s.mask)
        s.kept, s.total = found[4:]
        s.heads = exchange(found[:4])
    for m in range(micros):
        s = state[m]
        s.mixed, *parts = output_part(ids, s.heads, held["o"])
        s.middle, low_two = middle_norm(
            *reduce_rows(parts), s.own, output_shift, gain_two, bias_two
        )
        s.spread = spread_rows(low_two)
    for m in range(micros):
        s = state[m]
        found = feed(s.spread, s.low, held["i"], held["f"], inner_shift)
        s.normed_two, s.active, s.inner, s.inner_sum = found[:4]
        s.forward = found[4:8]
        s.final_own = s.low[:quarter]
        s.keep_two = reduce_rows(found[8:])

    def weight_grad(lefts, rights):
        if paired:
            away = sum(dot_tn(a[:, half:], b) for a, b in zip(lefts, rights))
            came = mate(away.astype(BF))
            home = sum(dot_tn(a[:, :half], b) for a, b in zip(lefts, rights))
            return home, came
        full = sum(dot_tn(a, b) for a, b in zip(lefts, rights))
        return lax.psum_scatter(
            full.astype(BF), "shard", scatter_dimension=0, tiled=True
        ), None

    def joined(pair):
        home, came = pair
        return home if came is None else (home + came.astype(F32)).astype(BF)

    inner_pair = (ctx_at == 1) | (ctx_at == 2)
    hops = ([(0, 1), (3, 2)], [(1, 2), (2, 1)], [(1, 0), (2, 3)])

    def hop(stage, values):
        return [lax.ppermute(v, "ctx", hops[stage]) for v in values]

    def plus(values, others):
        return [(a.astype(F32) + b.astype(F32)).astype(BF) for a, b in zip(values, others)]

    def finish(whole, third):
        done = [jnp.where(inner_pair, a, b).astype(F32) for a, b in zip(whole, third)]
        return done[0] if len(done) == 1 else jnp.concatenate(done, 0)

    def cut(value, count):
        step = value.shape[0] // count
        return [value[i * step : (i + 1) * step] for i in range(count)]

    def tied(values, *others):
        return list(lax.optimization_barrier((tuple(values),) + others)[0])

    grads = {}
    pieces = 2 if (width // shard_count) % 32 == 0 else 1
    every = lambda name: [getattr(s, name) for s in state]
    outer = weight_grad(every("low"), every("active"))
    inner = weight_grad(every("normed_two"), every("inner"))
    for m in range(micros):
        s = state[m]
        found = middle_back(*s.keep_two, s.middle, s.final_own, gain_two)
        s.grad_middle, low_middle, s.gain_two, s.bias_two, s.shift_out = found
        s.low_parts = spread_rows(low_middle)
    outer = cut(joined(outer), pieces)
    outer_first = hop(0, outer)
    for m in range(micros):
        s = state[m]
        parts = s.low_parts if m else tied(s.low_parts, outer)
        s.low_middle, *slabs = attended_grad(ids, parts, held["o"])
        s.head_grads = exchange(slabs)
    output = weight_grad(every("low_middle"), every("mixed"))
    for m in range(micros):
        s = state[m]
        s.slabs_back = attend_back(
            s.plan, s.slabs, s.head_grads, s.kept, s.total, s.mask
        )
        s.back = exchange(s.slabs_back)
    inner = cut(joined(inner), pieces)
    output = [joined(output)]
    outer = plus(outer, outer_first)
    inner_first = hop(0, inner)
    outer_second = hop(1, outer)
    output_first = hop(0, output)
    last = micros - 1
    for m in range(micros):
        s = state[m]
        back = s.back if m != last else tied(s.back, inner, outer, output)
        found = project_back(ids, back, qkv)
        s.gq, s.gk, s.gv, s.q_sum, s.v_sum = found[:5]
        s.keep_one = reduce_rows(found[5:])
    names = "kvq"
    three = {
        n: weight_grad(every("normed"), every(g)) for n, g in zip(names, ("gk", "gv", "gq"))
    }
    for m in range(micros):
        s = state[m]
        out, s.gain_one, s.bias_one = first_back(
            *s.keep_one, s.own, s.grad_middle, gain_one
        )
        s.frames_grad = spread_rows(out)
    outer = plus(outer, outer_second)
    inner = plus(inner, inner_first)
    output = plus(output, output_first)
    outer_third = hop(2, outer)
    inner_second = hop(1, inner)
    output_second = hop(1, output)
    three = {n: tied([joined(three[n])], inner, outer, output) for n in names}
    three_first = {n: hop(0, three[n]) for n in names}
    inner = plus(inner, inner_second)
    output = plus(output, output_second)
    inner_third = hop(2, inner)
    output_third = hop(2, output)
    three = {n: plus(three[n], three_first[n]) for n in names}
    three_second = {n: hop(1, three[n]) for n in names}
    three = {n: plus(three[n], three_second[n]) for n in names}
    for n in names:
        grads[n] = finish(three[n], hop(2, three[n]))
    grads["f"] = finish(outer, outer_third)
    grads["i"] = finish(inner, inner_third)
    grads["o"] = finish(output, output_third)
    for m in range(micros):
        s = state[m]
        keep, near, far = reduce_rows(tied(s.forward, state[last].slabs_back[0]))
        final = (
            s.middle + (keep + near.astype(F32) + far.astype(F32)) + outer_shift
        ).astype(BF)
        s.result = spread_rows(final)
    result = gather_rows(ids, sum((s.result for s in state), ()))
    frames_grad = gather_rows(ids, sum((s.frames_grad for s in state), ()))

    def over_all(value):
        value = value + core(value)
        return value + across(value)

    def over_frames(value):
        value = value + mate(value) if paired else lax.psum(value, "shard")
        value = value + blocks(value, 1)
        return value + blocks(value, 2)

    def both(name):
        return sum(every(name))

    shift_final = sum(
        jnp.sum(s.final_own.astype(F32), 0, keepdims=True) for s in state
    )
    small = jnp.concatenate(
        [
            turn(both("gain_one")),
            turn(both("bias_one")),
            turn(both("gain_two")),
            turn(both("bias_two")),
            turn(both("shift_out")),
            turn(shift_final),
        ],
        0,
    )
    small = over_all(small)
    group = query_weight.shape[1]
    hidden = inner_weight.shape[1]
    narrow = jnp.concatenate([both("inner_sum"), both("q_sum"), both("v_sum")], 1)
    room = -narrow.shape[1] % width
    narrow = jnp.pad(narrow, ((0, 0), (0, room))).reshape(-1, width)
    small = over_frames(jnp.concatenate([small, narrow], 0))
    narrow = small[6:].reshape(-1)
    return (
        result,
        frames_grad,
        small[0],
        small[1],
        grads["q"],
        narrow[hidden : hidden + group],
        grads["k"],
        grads["v"],
        narrow[hidden + group : hidden + 2 * group],
        grads["o"],
        small[4],
        small[2],
        small[3],
        grads["i"],
        narrow[:hidden],
        grads["f"],
        small[5],
    )


def layer(sizes, *arrays):
    return per_device(sizes, *arrays)


def solution(mesh):
    split = P(None, "shard", "ctx", None)
    cut = P("shard", "tp")
    ins = (split, P(None, "shard"), P(), P(), cut, P("tp"), cut, cut, P("tp"), cut)
    ins += (P(), P(), P(), cut, P("tp"), cut, P(), split)
    outs = (split, split, P(), P(), cut, P("tp"), cut, cut, P("tp"), cut)
    outs += (P(), P(), P(), cut, P("tp"), cut, P())
    return jax.shard_map(
        functools.partial(layer, dict(mesh.shape)),
        mesh=mesh,
        in_specs=ins,
        out_specs=outs,
        check_vma=False,
    )
```

profile of v0, /device:TPU:0, one launch (start us, length us, event | category | flops | bytes accessed | tf_op | source)
XLA Modules:
  0.0 710.2 jit_solution(9618286524461758385)
XLA Ops:
  26.5 5.4 shard_map.311
  32.7 4.9 collective-permute-done.2.vb
  37.6 5.7 shard_map.312
  54.7 10.9 %collective-permute-done.19.x2 = bf16[240,512]{1,0:T(8,128)(2,1)S(1)} collective-permute-done((bf16[240,512]{1,0:T(8,128)(2,1)}, bf16[240,512]{1,0:T(8,128)(2,1)S(1)}, u32[]{:S(2)}, u32[]{:S(2)}) %collective-permute-start.19) | collective-permute-done | bytes 245792 | tf_op jit(solution)/shard_map/ppermute | solution.py:623
  66.4 9.8 %shard_map.313 = (bf16[80,512]{1,0:T(8,128)(2,1)}, bf16[80,512]{1,0:T(8,128)(2,1)}, bf16[80,512]{1,0:T(8,128)(2,1)}, bf16[80,512]{1,0:T(8,128)(2,1)}, f32[4,80,512]{2,1,0:T(8,128)}, /*index=5*/f32[4,1,512]{2,1,0:T(1,128)}) custom-call(s32[5]{0:T(128)} %pad_add_fusion.4.plan, bf16[240,512]{1,0:T(8,128)(2,1)} %get-tuple-element.177.x0, ...), custom_call_target="tpu_custom_call" | custom-call | tf_op jit(solution)/shard_map/pallas_call | solution.py:172
  80.3 5.4 shard_map.305
  85.8 5.7 shard_map.306
  97.2 20.7 %collective-permute-done.22.m2 = bf16[80,512]{1,0:T(8,128)(2,1)S(1)} collective-permute-done((bf16[80,512]{1,0:T(8,128)(2,1)S(1)}, bf16[80,512]{1,0:T(8,128)(2,1)S(1)}, u32[]{:S(2)}, u32[]{:S(2)}) %collective-permute-start.22) | collective-permute-done | bytes 81952 | tf_op jit(solution)/shard_map/ppermute | solution.py:623
  125.5 3.7 shard_map.314
  134.7 3.6 collective-permute-start.7
  147.6 3.6 shard_map.308
  157.7 6.5 collective-permute-done.26.second
  178.8 5.9 collective-permute-done.13.n1
  184.8 33.2 %collective-permute-done.17.ob = bf16[640,1280]{1,0:T(8,128)(2,1)} collective-permute-done((bf16[640,1280]{1,0:T(8,128)(2,1)}, bf16[640,1280]{1,0:T(8,128)(2,1)}, u32[]{:S(2)}, u32[]{:S(2)}) %collective-permute-start.17) | collective-permute-done | bytes 1638432 | tf_op jit(solution)/shard_map/ppermute | solution.py:626
  218.7 15.9 %shard_map.316 = (bf16[512,1280]{1,0:T(8,128)(2,1)}, bf16[512,1280]{1,0:T(8,128)(2,1)}, bf16[512,1280]{1,0:T(8,128)(2,1)}, f32[1,1280]{1,0:T(1,128)}, f32[128,12...) custom-call(bf16[128,1280]{1,0:T(8,128)(2,1)} %get-tuple-element.189, ...), custom_call_target="tpu_custom_call" | custom-call | tf_op jit(solution)/shard_map/pallas_call | solution.py:408
  236.0 16.4 %shard_map.310 = (bf16[512,1280]{1,0:T(8,128)(2,1)}, bf16[512,1280]{1,0:T(8,128)(2,1)}, bf16[512,1280]{1,0:T(8,128)(2,1)}, f32[1,1280]{1,0:T(1,128)}, f32[128,12...) custom-call(bf16[128,1280]{1,0:T(8,128)(2,1)} %get-tuple-element.168, ...), custom_call_target="tpu_custom_call" | custom-call | tf_op jit(solution)/shard_map/pallas_call | solution.py:408
  270.9 6.4 collective-permute-done.32.second
  296.8 3.5 collective-permute-start.37
  305.5 3.6 collective-permute-done.38.g3
  309.8 16.1 %shard_map.319 = (bf16[240,512]{1,0:T(8,128)(2,1)}, bf16[240,512]{1,0:T(8,128)(2,1)}, bf16[240,512]{1,0:T(8,128)(2,1)}, bf16[240,512]{1,0:T(8,128)(2,1)}) custom-call(s32[5]{0:T(128)} %pad_add_fusion.4.plan, bf16[240,512]{1,0:T(8,128)(2,1)} %get-tuple-element.177.x0, bf16[240,512]{1,0:T(8,128)(2,1)} %copy-done.45, bf16[240,512]{1,0:T(8,128)(2,1)} %copy-done.46, ...), custom_call_target="tpu_custom_call" | custom-call | tf_op jit(solution)/shard_map/pallas_call | solution.py:264
  326.3 4.1 fusion.5
  336.9 4.3 fusion.4
  349.2 3.8 shard_map.323
  357.2 4.0 collective-permute-done.61.s1
  363.3 12.0 %collective-permute-done.62.s2 = bf16[240,512]{1,0:T(8,128)(2,1)S(1)} collective-permute-done((bf16[240,512]{1,0:T(8,128)(2,1)S(1)}, bf16[240,512]{1,0:T(8,128)(2,1)S(1)}, u32[]{:S(2)}, u32[]{:S(2)}) %collective-permute-start.62) | collective-permute-done | bytes 245792 | tf_op jit(solution)/shard_map/ppermute | solution.py:623
  376.8 8.3 %collective-permute-done.63.s3 = bf16[240,512]{1,0:T(8,128)(2,1)S(1)} collective-permute-done((bf16[240,512]{1,0:T(8,128)(2,1)S(1)}, bf16[240,512]{1,0:T(8,128)(2,1)S(1)}, u32[]{:S(2)}, u32[]{:S(2)}) %collective-permute-start.63) | collective-permute-done | bytes 245792 | tf_op jit(solution)/shard_map/ppermute | solution.py:623
  386.8 6.0 shard_map.324
  400.0 7.7 %collective-permute-done.76 = bf16[640,320]{0,1:T(8,128)(2,1)S(1)} collective-permute-done((bf16[640,320]{0,1:T(8,128)(2,1)}, bf16[640,320]{0,1:T(8,128)(2,1)S(1)}, u32[]{:S(2)}, u32[]{:S(2)}) %collective-permute-start.76) | collective-permute-done | bytes 409632 | tf_op jit(solution)/shard_map/ppermute | solution.py:626
  414.3 5.2 collective-permute-start.90
  419.5 12.4 %collective-permute-done.74 = bf16[320,1280]{1,0:T(8,128)(2,1)S(1)} collective-permute-done((bf16[320,1280]{1,0:T(8,128)(2,1)}, bf16[320,1280]{1,0:T(8,128)(2,1)S(1)}, u32[]{:S(2)}, u32[]{:S(2)}) %collective-permute-start.74) | collective-permute-done | bytes 819232 | tf_op jit(solution)/shard_map/ppermute | solution.py:760
  431.9 5.4 collective-permute-start.89
  438.9 6.5 collective-permute-done.72.s3
  446.1 6.0 shard_map.326
  460.5 3.8 collective-permute-start.93
  464.4 13.1 %collective-permute-done.89 = bf16[320,1280]{1,0:T(8,128)(2,1)} collective-permute-done((bf16[320,1280]{1,0:T(8,128)(2,1)}, bf16[320,1280]{1,0:T(8,128)(2,1)}, u32[]{:S(2)}, u32[]{:S(2)}) %collective-permute-start.89) | collective-permute-done | bytes 819232 | tf_op jit(solution)/shard_map/ppermute | solution.py:760
  486.6 7.5 %collective-permute-done.48.refs_5_ = bf16[128,1280]{1,0:T(8,128)(2,1)} collective-permute-done((bf16[128,1280]{1,0:T(8,128)(2,1)}, bf16[128,1280]{1,0:T(8,128)(2,1)}, u32[]{:S(2)}, u32[]{:S(2)}) %collective-permute-start.48) | collective-permute-done | bytes 327712 | tf_op jit(solution)/shard_map/ppermute | solution.py:620
  494.7 5.9 collective-permute-done.66.second
  509.9 5.7 shard_map.320
  525.9 5.4 collective-permute-done.97
  543.5 15.1 %collective-permute-start.86 = (f32[8,1280]{1,0:T(8,128)S(1)}, f32[8,1280]{1,0:T(8,128)S(1)}, u32[]{:S(2)}, u32[]{:S(2)}) collective-permute-start(f32[8,1280]{1,0:T(8,128)S(1)} %add.329), channel_id=1, source_target_pairs={{0,4},{4,0},{8,12},{12,8},{1,5},{5,1},{9,13},{13,9},{2,6},{6,2},{1... | collective-permute-start | bytes 122888 | tf_op jit(solution)/shard_map/ppermute | solution.py:623
  566.7 10.7 %collective-permute-start.87 = (f32[8,1280]{1,0:T(8,128)S(1)}, f32[8,1280]{1,0:T(8,128)S(1)}, u32[]{:S(2)}, u32[]{:S(2)}) collective-permute-start(f32[8,1280]{1,0:T(8,128)S(1)} %add.330), channel_id=1, source_target_pairs={{0,8},{4,12},{8,0},{12,4},{1,9},{5,13},{9,1},{13,5},{2,10},{6,14},... | collective-permute-start | bytes 122888 | tf_op jit(solution)/shard_map/ppermute | solution.py:623
  577.6 18.8 %collective-permute-start.94 = (bf16[640,320]{0,1:T(8,128)(2,1)}, bf16[640,320]{0,1:T(8,128)(2,1)}, u32[]{:S(2)}, u32[]{:S(2)}) collective-permute-start(bf16[640,320]{0,1:T(8,128)(2,1)} %fusion.15), channel_id=1, source_target_pairs={{0,4},{12,8},{1,5},{13,9},{2,6},{14,10},{3,7},{15,11},{16,20},{28,... | collective-permute-start | bytes 1228808 | tf_op jit(solution)/shard_map/ppermute | solution.py:760
  610.3 4.3 collective-permute-done.98
  614.6 6.2 collective-permute-done.102
  630.8 5.7 shard_map.328
  643.4 39.5 %collective-permute-done.108 = bf16[320,1280]{1,0:T(8,128)(2,1)} collective-permute-done((bf16[320,1280]{1,0:T(8,128)(2,1)S(1)}, bf16[320,1280]{1,0:T(8,128)(2,1)}, u32[]{:S(2)}, u32[]{:S(2)}) %collective-permute-start.108) | collective-permute-done | bytes 819232 | tf_op jit(solution)/shard_map/ppermute | solution.py:760
  692.8 7.5 %collective-permute-done.100 = bf16[640,320]{0,1:T(8,128)(2,1)S(1)} collective-permute-done((bf16[640,320]{0,1:T(8,128)(2,1)S(1)}, bf16[640,320]{0,1:T(8,128)(2,1)S(1)}, u32[]{:S(2)}, u32[]{:S(2)}) %collective-permute-start.100) | collective-permute-done | bytes 409632 | tf_op jit(solution)/shard_map/ppermute | solution.py:760
  701.3 7.5 %collective-permute-done.104 = bf16[640,320]{0,1:T(8,128)(2,1)S(1)} collective-permute-done((bf16[640,320]{0,1:T(8,128)(2,1)S(1)}, bf16[640,320]{0,1:T(8,128)(2,1)S(1)}, u32[]{:S(2)}, u32[]{:S(2)}) %collective-permute-start.104) | collective-permute-done | bytes 409632 | tf_op jit(solution)/shard_map/ppermute | solution.py:760
  (595 shorter events, 278.4 us)
Async XLA Ops:
  2.1 30.5 %collective-permute-start = (bf16[640,320]{1,0:T(8,128)(2,1)S(1)}, bf16[640,320]{1,0:T(8,128)(2,1)}, u32[]{:S(2)}, u32[]{:S(2)}) collective-permute-start(bf16[640,320]{1,0:T(8,128)(2,1)S(1)} %copy.58.qa), channel_id=1, source_target_pairs={{0,16},{16,0},{1,17},{17,1},{2,18},{18,2},{3,19},{19,3},{4,20},{20... | collective-permute-start | bytes 1228808 | tf_op jit(solution)/shard_map/ppermute | solution.py:626
  9.3 28.3 %collective-permute-start.2 = (bf16[640,320]{1,0:T(8,128)(2,1)}, bf16[640,320]{1,0:T(8,128)(2,1)}, u32[]{:S(2)}, u32[]{:S(2)}) collective-permute-start(bf16[640,320]{1,0:T(8,128)(2,1)} %copy.60.va), channel_id=1, source_target_pairs={{0,16},{16,0},{1,17},{17,1},{2,18},{18,2},{3,19},{19,3},{4,20},{20... | collective-permute-start | bytes 1228808 | tf_op jit(solution)/shard_map/ppermute | solution.py:626
  50.9 73.2 %collective-permute-start.9 = (bf16[640,320]{1,0:T(8,128)(2,1)S(1)}, bf16[640,320]{1,0:T(8,128)(2,1)S(1)}, u32[]{:S(2)}, u32[]{:S(2)}) collective-permute-start(bf16[640,320]{1,0:T(8,128)(2,1)S(1)} %copy.61), channel_id=1, source_target_pairs={{0,16},{16,0},{1,17},{17,1},{2,18},{18,2},{3,19},{19,3},{4,20},{20... | collective-permute-start | bytes 1228808 | tf_op jit(solution)/shard_map/ppermute | solution.py:626
  91.4 39.7 %collective-permute-start.3 = (bf16[240,512]{1,0:T(8,128)(2,1)}, bf16[240,512]{1,0:T(8,128)(2,1)S(1)}, u32[]{:S(2)}, u32[]{:S(2)}) collective-permute-start(bf16[240,512]{1,0:T(8,128)(2,1)} %get-tuple-element.155), channel_id=1, source_target_pairs={{0,4},{4,0},{8,12},{12,8},{1,5},{5,1},{9,13},{13,9},{2,6},{6,2},{1... | collective-permute-start | bytes 737288 | tf_op jit(solution)/shard_map/ppermute | solution.py:623
  91.5 39.7 %collective-permute-start.4 = (bf16[240,512]{1,0:T(8,128)(2,1)}, bf16[240,512]{1,0:T(8,128)(2,1)}, u32[]{:S(2)}, u32[]{:S(2)}) collective-permute-start(bf16[240,512]{1,0:T(8,128)(2,1)} %get-tuple-element.156), channel_id=1, source_target_pairs={{0,8},{4,12},{8,0},{12,4},{1,9},{5,13},{9,1},{13,5},{2,10},{6,14},... | collective-permute-start | bytes 737288 | tf_op jit(solution)/shard_map/ppermute | solution.py:623
  94.6 36.6 %collective-permute-start.5 = (bf16[240,512]{1,0:T(8,128)(2,1)}, bf16[240,512]{1,0:T(8,128)(2,1)}, u32[]{:S(2)}, u32[]{:S(2)}) collective-permute-start(bf16[240,512]{1,0:T(8,128)(2,1)} %get-tuple-element.157), channel_id=1, source_target_pairs={{0,12},{4,8},{8,4},{12,0},{1,13},{5,9},{9,5},{13,1},{2,14},{6,10},... | collective-permute-start | bytes 737288 | tf_op jit(solution)/shard_map/ppermute | solution.py:623
  143.6 41.1 %collective-permute-start.16 = (bf16[640,1280]{1,0:T(8,128)(2,1)}, bf16[640,1280]{1,0:T(8,128)(2,1)}, u32[]{:S(2)}, u32[]{:S(2)}) collective-permute-start(bf16[640,1280]{1,0:T(8,128)(2,1)} %ia.3), channel_id=1, source_target_pairs={{0,16},{16,0},{1,17},{17,1},{2,18},{18,2},{3,19},{19,3},{4,20},{20... | collective-permute-start | bytes 4915208 | tf_op jit(solution)/shard_map/ppermute | solution.py:626
  146.9 71.1 %collective-permute-start.17 = (bf16[640,1280]{1,0:T(8,128)(2,1)}, bf16[640,1280]{1,0:T(8,128)(2,1)}, u32[]{:S(2)}, u32[]{:S(2)}) collective-permute-start(bf16[640,1280]{1,0:T(8,128)(2,1)} %oa.3), channel_id=1, source_target_pairs={{0,16},{16,0},{1,17},{17,1},{2,18},{18,2},{3,19},{19,3},{4,20},{20... | collective-permute-start | bytes 4915208 | tf_op jit(solution)/shard_map/ppermute | solution.py:626
  178.3 56.9 %collective-permute-start.14 = (bf16[128,1280]{1,0:T(8,128)(2,1)}, bf16[128,1280]{1,0:T(8,128)(2,1)S(1)}, u32[]{:S(2)}, u32[]{:S(2)}) collective-permute-start(bf16[128,1280]{1,0:T(8,128)(2,1)} %get-tuple-element.168.n0), channel_id=1, source_target_pairs={{0,1},{1,0},{2,3},{3,2},{4,5},{5,4},{6,7},{7,6},{8,9},{9,8},{10,11... | collective-permute-start | bytes 983048 | tf_op jit(solution)/shard_map/ppermute | solution.py:617
  178.3 39.7 %collective-permute-start.29 = (bf16[128,1280]{1,0:T(8,128)(2,1)S(1)}, bf16[128,1280]{1,0:T(8,128)(2,1)S(1)}, u32[]{:S(2)}, u32[]{:S(2)}) collective-permute-start(bf16[128,1280]{1,0:T(8,128)(2,1)S(1)} %collective-permute-done.27.n1), channel_id=1, source_target_pairs={{0,1},{1,0},{2,3},{3,2},{4,5},{5,4},{6,7},{7,6},{8,9},{9,8},{10,11... | collective-permute-start | bytes 983048 | tf_op jit(solution)/shard_map/ppermute | solution.py:617
  184.7 50.5 %collective-permute-start.15 = (bf16[128,1280]{1,0:T(8,128)(2,1)S(1)}, bf16[128,1280]{1,0:T(8,128)(2,1)}, u32[]{:S(2)}, u32[]{:S(2)}) collective-permute-start(bf16[128,1280]{1,0:T(8,128)(2,1)S(1)} %collective-permute-done.13.n1), channel_id=1, source_target_pairs={{0,1},{1,0},{2,3},{3,2},{4,5},{5,4},{6,7},{7,6},{8,9},{9,8},{10,11... | collective-permute-start | bytes 983048 | tf_op jit(solution)/shard_map/ppermute | solution.py:617
  234.6 35.9 %collective-permute-start.30 = (bf16[128,1280]{1,0:T(8,128)(2,1)}, bf16[128,1280]{1,0:T(8,128)(2,1)}, u32[]{:S(2)}, u32[]{:S(2)}) collective-permute-start(bf16[128,1280]{1,0:T(8,128)(2,1)} %get-tuple-element.192), channel_id=1, source_target_pairs={{0,1},{1,0},{2,3},{3,2},{4,5},{5,4},{6,7},{7,6},{8,9},{9,8},{10,11... | collective-permute-start | bytes 983048 | tf_op jit(solution)/shard_map/ppermute | solution.py:617
  234.7 30.7 %collective-permute-start.31 = (bf16[128,1280]{1,0:T(8,128)(2,1)}, bf16[128,1280]{1,0:T(8,128)(2,1)}, u32[]{:S(2)}, u32[]{:S(2)}) collective-permute-start(bf16[128,1280]{1,0:T(8,128)(2,1)} %get-tuple-element.194), channel_id=1, source_target_pairs={{0,1},{1,0},{2,3},{3,2},{4,5},{5,4},{6,7},{7,6},{8,9},{9,8},{10,11... | collective-permute-start | bytes 983048 | tf_op jit(solution)/shard_map/ppermute | solution.py:617
  252.4 30.4 %collective-permute-start.51 = (bf16[128,1280]{1,0:T(8,128)(2,1)}, bf16[128,1280]{1,0:T(8,128)(2,1)}, u32[]{:S(2)}, u32[]{:S(2)}) collective-permute-start(bf16[128,1280]{1,0:T(8,128)(2,1)} %get-tuple-element.217), channel_id=1, source_target_pairs={{0,1},{1,0},{2,3},{3,2},{4,5},{5,4},{6,7},{7,6},{8,9},{9,8},{10,11... | collective-permute-start | bytes 983048 | tf_op jit(solution)/shard_map/ppermute | solution.py:617
  256.9 68.9 %collective-permute-start.57 = (bf16[640,1280]{1,0:T(8,128)(2,1)}, bf16[640,1280]{1,0:T(8,128)(2,1)}, u32[]{:S(2)}, u32[]{:S(2)}) collective-permute-start(bf16[640,1280]{1,0:T(8,128)(2,1)} %fusion.2), channel_id=1, source_target_pairs={{0,16},{16,0},{1,17},{17,1},{2,18},{18,2},{3,19},{19,3},{4,20},{20... | collective-permute-start | bytes 4915208 | tf_op jit(solution)/shard_map/ppermute | solution.py:626
  270.5 65.0 %collective-permute-start.73 = (bf16[640,1280]{1,0:T(8,128)(2,1)}, bf16[640,1280]{1,0:T(8,128)(2,1)}, u32[]{:S(2)}, u32[]{:S(2)}) collective-permute-start(bf16[640,1280]{1,0:T(8,128)(2,1)} %fusion.3), channel_id=1, source_target_pairs={{0,16},{16,0},{1,17},{17,1},{2,18},{18,2},{3,19},{19,3},{4,20},{20... | collective-permute-start | bytes 4915208 | tf_op jit(solution)/shard_map/ppermute | solution.py:626
  305.0 27.1 %collective-permute-start.55 = (bf16[128,1280]{1,0:T(8,128)(2,1)}, bf16[128,1280]{1,0:T(8,128)(2,1)}, u32[]{:S(2)}, u32[]{:S(2)}) collective-permute-start(bf16[128,1280]{1,0:T(8,128)(2,1)} %get-tuple-element.223.l0), channel_id=1, source_target_pairs={{0,1},{1,0},{2,3},{3,2},{4,5},{5,4},{6,7},{7,6},{8,9},{9,8},{10,11... | collective-permute-start | bytes 983048 | tf_op jit(solution)/shard_map/ppermute | solution.py:617
  305.0 27.2 %collective-permute-start.56 = (bf16[128,1280]{1,0:T(8,128)(2,1)}, bf16[128,1280]{1,0:T(8,128)(2,1)}, u32[]{:S(2)}, u32[]{:S(2)}) collective-permute-start(bf16[128,1280]{1,0:T(8,128)(2,1)} %collective-permute-done.54.l1), channel_id=1, source_target_pairs={{0,1},{1,0},{2,3},{3,2},{4,5},{5,4},{6,7},{7,6},{8,9},{9,8},{10,11... | collective-permute-start | bytes 983048 | tf_op jit(solution)/shard_map/ppermute | solution.py:617
  325.8 67.0 %collective-permute-start.45 = (bf16[128,1280]{1,0:T(8,128)(2,1)}, bf16[128,1280]{1,0:T(8,128)(2,1)}, u32[]{:S(2)}, u32[]{:S(2)}) collective-permute-start(bf16[128,1280]{1,0:T(8,128)(2,1)} %get-tuple-element.213), channel_id=1, source_target_pairs={{0,1},{1,0},{2,3},{3,2},{4,5},{5,4},{6,7},{7,6},{8,9},{9,8},{10,11... | collective-permute-start | bytes 983048 | tf_op jit(solution)/shard_map/ppermute | solution.py:617
  346.0 49.5 %collective-permute-start.39 = (bf16[128,1280]{1,0:T(8,128)(2,1)}, bf16[128,1280]{1,0:T(8,128)(2,1)}, u32[]{:S(2)}, u32[]{:S(2)}) collective-permute-start(bf16[128,1280]{1,0:T(8,128)(2,1)} %get-tuple-element.205), channel_id=1, source_target_pairs={{0,1},{1,0},{2,3},{3,2},{4,5},{5,4},{6,7},{7,6},{8,9},{9,8},{10,11... | collective-permute-start | bytes 983048 | tf_op jit(solution)/shard_map/ppermute | solution.py:617
  346.1 50.7 %collective-permute-start.47 = (bf16[128,1280]{1,0:T(8,128)(2,1)}, bf16[128,1280]{1,0:T(8,128)(2,1)}, u32[]{:S(2)}, u32[]{:S(2)}) collective-permute-start(bf16[128,1280]{1,0:T(8,128)(2,1)} %add_convert_fusion.20), channel_id=1, source_target_pairs={{0,2},{1,3},{2,0},{3,1},{4,6},{5,7},{6,4},{7,5},{8,10},{9,11},{10,... | collective-permute-start | bytes 983048 | tf_op jit(solution)/shard_map/ppermute | solution.py:620
  354.8 42.1 %collective-permute-start.41 = (bf16[128,1280]{1,0:T(8,128)(2,1)}, bf16[128,1280]{1,0:T(8,128)(2,1)}, u32[]{:S(2)}, u32[]{:S(2)}) collective-permute-start(bf16[128,1280]{1,0:T(8,128)(2,1)} %add_convert_fusion.22), channel_id=1, source_target_pairs={{0,2},{1,3},{2,0},{3,1},{4,6},{5,7},{6,4},{7,5},{8,10},{9,11},{10,... | collective-permute-start | bytes 983048 | tf_op jit(solution)/shard_map/ppermute | solution.py:620
  385.1 53.6 %collective-permute-start.70 = (bf16[240,512]{1,0:T(8,128)(2,1)}, bf16[240,512]{1,0:T(8,128)(2,1)}, u32[]{:S(2)}, u32[]{:S(2)}) collective-permute-start(bf16[240,512]{1,0:T(8,128)(2,1)} %get-tuple-element.243), channel_id=1, source_target_pairs={{0,4},{4,0},{8,12},{12,8},{1,5},{5,1},{9,13},{13,9},{2,6},{6,2},{1... | collective-permute-start | bytes 737288 | tf_op jit(solution)/shard_map/ppermute | solution.py:623
  395.5 36.4 %collective-permute-start.74 = (bf16[320,1280]{1,0:T(8,128)(2,1)}, bf16[320,1280]{1,0:T(8,128)(2,1)S(1)}, u32[]{:S(2)}, u32[]{:S(2)}) collective-permute-start(bf16[320,1280]{1,0:T(8,128)(2,1)} %get-tuple-element.323), channel_id=1, source_target_pairs={{0,4},{12,8},{1,5},{13,9},{2,6},{14,10},{3,7},{15,11},{16,20},{28,... | collective-permute-start | bytes 2457608 | tf_op jit(solution)/shard_map/ppermute | solution.py:760
  407.6 31.0 %collective-permute-start.71 = (bf16[240,512]{1,0:T(8,128)(2,1)S(1)}, bf16[240,512]{1,0:T(8,128)(2,1)S(1)}, u32[]{:S(2)}, u32[]{:S(2)}) collective-permute-start(bf16[240,512]{1,0:T(8,128)(2,1)S(1)} %copy-done.113), channel_id=1, source_target_pairs={{0,8},{4,12},{8,0},{12,4},{1,9},{5,13},{9,1},{13,5},{2,10},{6,14},... | collective-permute-start | bytes 737288 | tf_op jit(solution)/shard_map/ppermute | solution.py:623
  409.4 36.1 %collective-permute-start.72 = (bf16[240,512]{1,0:T(8,128)(2,1)S(1)}, bf16[240,512]{1,0:T(8,128)(2,1)S(1)}, u32[]{:S(2)}, u32[]{:S(2)}) collective-permute-start(bf16[240,512]{1,0:T(8,128)(2,1)S(1)} %copy-done.112), channel_id=1, source_target_pairs={{0,12},{4,8},{8,4},{12,0},{1,13},{5,9},{9,5},{13,1},{2,14},{6,10},... | collective-permute-start | bytes 737288 | tf_op jit(solution)/shard_map/ppermute | solution.py:623
  414.3 46.2 %collective-permute-start.90 = (bf16[320,1280]{1,0:T(8,128)(2,1)}, bf16[320,1280]{1,0:T(8,128)(2,1)}, u32[]{:S(2)}, u32[]{:S(2)}) collective-permute-start(bf16[320,1280]{1,0:T(8,128)(2,1)} %get-tuple-element.320), channel_id=1, source_target_pairs={{0,4},{12,8},{1,5},{13,9},{2,6},{14,10},{3,7},{15,11},{16,20},{28,... | collective-permute-start | bytes 2457608 | tf_op jit(solution)/shard_map/ppermute | solution.py:760
  431.9 45.6 %collective-permute-start.89 = (bf16[320,1280]{1,0:T(8,128)(2,1)}, bf16[320,1280]{1,0:T(8,128)(2,1)}, u32[]{:S(2)}, u32[]{:S(2)}) collective-permute-start(bf16[320,1280]{1,0:T(8,128)(2,1)} %get-tuple-element.321), channel_id=1, source_target_pairs={{0,4},{12,8},{1,5},{13,9},{2,6},{14,10},{3,7},{15,11},{16,20},{28,... | collective-permute-start | bytes 2457608 | tf_op jit(solution)/shard_map/ppermute | solution.py:760
  438.6 44.5 %collective-permute-start.64 = (bf16[128,1280]{1,0:T(8,128)(2,1)}, bf16[128,1280]{1,0:T(8,128)(2,1)}, u32[]{:S(2)}, u32[]{:S(2)}) collective-permute-start(bf16[128,1280]{1,0:T(8,128)(2,1)} %get-tuple-element.238), channel_id=1, source_target_pairs={{0,1},{1,0},{2,3},{3,2},{4,5},{5,4},{6,7},{7,6},{8,9},{9,8},{10,11... | collective-permute-start | bytes 983048 | tf_op jit(solution)/shard_map/ppermute | solution.py:617
  438.6 47.5 %collective-permute-start.42 = (bf16[128,1280]{1,0:T(8,128)(2,1)}, bf16[128,1280]{1,0:T(8,128)(2,1)}, u32[]{:S(2)}, u32[]{:S(2)}) collective-permute-start(bf16[128,1280]{1,0:T(8,128)(2,1)} %get-tuple-element.331.refs_0_), channel_id=1, source_target_pairs={{0,2},{1,3},{2,0},{3,1},{4,6},{5,7},{6,4},{7,5},{8,10},{9,11},{10,... | collective-permute-start | bytes 983048 | tf_op jit(solution)/shard_map/ppermute | solution.py:620
  445.4 40.7 %collective-permute-start.43 = (bf16[128,1280]{1,0:T(8,128)(2,1)}, bf16[128,1280]{1,0:T(8,128)(2,1)}, u32[]{:S(2)}, u32[]{:S(2)}) collective-permute-start(bf16[128,1280]{1,0:T(8,128)(2,1)} %get-tuple-element.331.refs_0_), channel_id=1, source_target_pairs={{0,1},{1,0},{2,3},{3,2},{4,5},{5,4},{6,7},{7,6},{8,9},{9,8},{10,11... | collective-permute-start | bytes 983048 | tf_op jit(solution)/shard_map/ppermute | solution.py:617
  460.5 33.6 %collective-permute-start.93 = (bf16[640,320]{0,1:T(8,128)(2,1)S(1)}, bf16[640,320]{0,1:T(8,128)(2,1)S(1)}, u32[]{:S(2)}, u32[]{:S(2)}) collective-permute-start(bf16[640,320]{0,1:T(8,128)(2,1)S(1)} %copy-done.31), channel_id=1, source_target_pairs={{0,4},{12,8},{1,5},{13,9},{2,6},{14,10},{3,7},{15,11},{16,20},{28,... | collective-permute-start | bytes 1228808 | tf_op jit(solution)/shard_map/ppermute | solution.py:760
  506.8 55.3 %collective-permute-start.91 = (bf16[320,1280]{1,0:T(8,128)(2,1)S(1)}, bf16[320,1280]{1,0:T(8,128)(2,1)}, u32[]{:S(2)}, u32[]{:S(2)}) collective-permute-start(bf16[320,1280]{1,0:T(8,128)(2,1)S(1)} %copy-done.17), channel_id=1, source_target_pairs={{4,8},{8,4},{5,9},{9,5},{6,10},{10,6},{7,11},{11,7},{20,24},{24,20... | collective-permute-start | bytes 2457608 | tf_op jit(solution)/shard_map/ppermute | solution.py:760
  508.3 56.3 %collective-permute-start.92 = (bf16[320,1280]{1,0:T(8,128)(2,1)S(1)}, bf16[320,1280]{1,0:T(8,128)(2,1)}, u32[]{:S(2)}, u32[]{:S(2)}) collective-permute-start(bf16[320,1280]{1,0:T(8,128)(2,1)S(1)} %get-tuple-element.318), channel_id=1, source_target_pairs={{4,8},{8,4},{5,9},{9,5},{6,10},{10,6},{7,11},{11,7},{20,24},{24,20... | collective-permute-start | bytes 2457608 | tf_op jit(solution)/shard_map/ppermute | solution.py:760
  535.3 31.3 %collective-permute-start.109 = (bf16[320,1280]{1,0:T(8,128)(2,1)S(1)}, bf16[320,1280]{1,0:T(8,128)(2,1)S(1)}, u32[]{:S(2)}, u32[]{:S(2)}) collective-permute-start(bf16[320,1280]{1,0:T(8,128)(2,1)S(1)} %copy-done.19), channel_id=1, source_target_pairs={{4,8},{8,4},{5,9},{9,5},{6,10},{10,6},{7,11},{11,7},{20,24},{24,20... | collective-permute-start | bytes 2457608 | tf_op jit(solution)/shard_map/ppermute | solution.py:760
  542.8 34.7 %collective-permute-start.107 = (bf16[320,1280]{1,0:T(8,128)(2,1)S(1)}, bf16[320,1280]{1,0:T(8,128)(2,1)S(1)}, u32[]{:S(2)}, u32[]{:S(2)}) collective-permute-start(bf16[320,1280]{1,0:T(8,128)(2,1)S(1)} %copy-done.18), channel_id=1, source_target_pairs={{4,8},{8,4},{5,9},{9,5},{6,10},{10,6},{7,11},{11,7},{20,24},{24,20... | collective-permute-start | bytes 2457608 | tf_op jit(solution)/shard_map/ppermute | solution.py:760
  560.6 49.1 %collective-permute-start.67 = (bf16[128,1280]{1,0:T(8,128)(2,1)}, bf16[128,1280]{1,0:T(8,128)(2,1)}, u32[]{:S(2)}, u32[]{:S(2)}) collective-permute-start(bf16[128,1280]{1,0:T(8,128)(2,1)} %get-tuple-element.242.refs_0_), channel_id=1, source_target_pairs={{0,2},{1,3},{2,0},{3,1},{4,6},{5,7},{6,4},{7,5},{8,10},{9,11},{10,... | collective-permute-start | bytes 983048 | tf_op jit(solution)/shard_map/ppermute | solution.py:620
  562.0 34.5 %collective-permute-start.106 = (bf16[640,320]{0,1:T(8,128)(2,1)S(1)}, bf16[640,320]{0,1:T(8,128)(2,1)S(1)}, u32[]{:S(2)}, u32[]{:S(2)}) collective-permute-start(bf16[640,320]{0,1:T(8,128)(2,1)S(1)} %add_convert_fusion.8), channel_id=1, source_target_pairs={{4,0},{8,12},{5,1},{9,13},{6,2},{10,14},{7,3},{11,15},{20,16},{24,... | collective-permute-start | bytes 1228808 | tf_op jit(solution)/shard_map/ppermute | solution.py:760
  564.7 45.0 %collective-permute-start.80 = (bf16[128,1280]{1,0:T(8,128)(2,1)}, bf16[128,1280]{1,0:T(8,128)(2,1)}, u32[]{:S(2)}, u32[]{:S(2)}) collective-permute-start(bf16[128,1280]{1,0:T(8,128)(2,1)} %get-tuple-element.263.refs_4_), channel_id=1, source_target_pairs={{0,2},{1,3},{2,0},{3,1},{4,6},{5,7},{6,4},{7,5},{8,10},{9,11},{10,... | collective-permute-start | bytes 983048 | tf_op jit(solution)/shard_map/ppermute | solution.py:620
  566.7 32.9 %collective-permute-start.87 = (f32[8,1280]{1,0:T(8,128)S(1)}, f32[8,1280]{1,0:T(8,128)S(1)}, u32[]{:S(2)}, u32[]{:S(2)}) collective-permute-start(f32[8,1280]{1,0:T(8,128)S(1)} %add.330), channel_id=1, source_target_pairs={{0,8},{4,12},{8,0},{12,4},{1,9},{5,13},{9,1},{13,5},{2,10},{6,14},... | collective-permute-start | bytes 122888 | tf_op jit(solution)/shard_map/ppermute | solution.py:623
  577.6 28.2 %collective-permute-start.94 = (bf16[640,320]{0,1:T(8,128)(2,1)}, bf16[640,320]{0,1:T(8,128)(2,1)}, u32[]{:S(2)}, u32[]{:S(2)}) collective-permute-start(bf16[640,320]{0,1:T(8,128)(2,1)} %fusion.15), channel_id=1, source_target_pairs={{0,4},{12,8},{1,5},{13,9},{2,6},{14,10},{3,7},{15,11},{16,20},{28,... | collective-permute-start | bytes 1228808 | tf_op jit(solution)/shard_map/ppermute | solution.py:760
  605.8 30.7 %collective-permute-start.110 = (bf16[320,1280]{1,0:T(8,128)(2,1)S(1)}, bf16[320,1280]{1,0:T(8,128)(2,1)}, u32[]{:S(2)}, u32[]{:S(2)}) collective-permute-start(bf16[320,1280]{1,0:T(8,128)(2,1)S(1)} %add_convert_fusion), channel_id=1, source_target_pairs={{4,0},{8,12},{5,1},{9,13},{6,2},{10,14},{7,3},{11,15},{20,16},{24,... | collective-permute-start | bytes 2457608 | tf_op jit(solution)/shard_map/ppermute | solution.py:760
  624.7 60.8 %collective-permute-start.112 = (bf16[320,1280]{1,0:T(8,128)(2,1)S(1)}, bf16[320,1280]{1,0:T(8,128)(2,1)}, u32[]{:S(2)}, u32[]{:S(2)}) collective-permute-start(bf16[320,1280]{1,0:T(8,128)(2,1)S(1)} %add_convert_fusion.2), channel_id=1, source_target_pairs={{4,0},{8,12},{5,1},{9,13},{6,2},{10,14},{7,3},{11,15},{20,16},{24,... | collective-permute-start | bytes 2457608 | tf_op jit(solution)/shard_map/ppermute | solution.py:760
  626.0 60.7 %collective-permute-start.111 = (bf16[320,1280]{1,0:T(8,128)(2,1)S(1)}, bf16[320,1280]{1,0:T(8,128)(2,1)}, u32[]{:S(2)}, u32[]{:S(2)}) collective-permute-start(bf16[320,1280]{1,0:T(8,128)(2,1)S(1)} %add_convert_fusion.3), channel_id=1, source_target_pairs={{4,0},{8,12},{5,1},{9,13},{6,2},{10,14},{7,3},{11,15},{20,16},{24,... | collective-permute-start | bytes 2457608 | tf_op jit(solution)/shard_map/ppermute | solution.py:760
  627.3 55.6 %collective-permute-start.108 = (bf16[320,1280]{1,0:T(8,128)(2,1)S(1)}, bf16[320,1280]{1,0:T(8,128)(2,1)}, u32[]{:S(2)}, u32[]{:S(2)}) collective-permute-start(bf16[320,1280]{1,0:T(8,128)(2,1)S(1)} %add_convert_fusion.1), channel_id=1, source_target_pairs={{4,0},{8,12},{5,1},{9,13},{6,2},{10,14},{7,3},{11,15},{20,16},{24,... | collective-permute-start | bytes 2457608 | tf_op jit(solution)/shard_map/ppermute | solution.py:760
  640.5 51.3 %collective-permute-start.96 = (bf16[640,320]{0,1:T(8,128)(2,1)S(1)}, bf16[640,320]{0,1:T(8,128)(2,1)S(1)}, u32[]{:S(2)}, u32[]{:S(2)}) collective-permute-start(bf16[640,320]{0,1:T(8,128)(2,1)S(1)} %add_convert_fusion.13), channel_id=1, source_target_pairs={{4,0},{8,12},{5,1},{9,13},{6,2},{10,14},{7,3},{11,15},{20,16},{24,... | collective-permute-start | bytes 1228808 | tf_op jit(solution)/shard_map/ppermute | solution.py:760
  642.0 58.4 %collective-permute-start.100 = (bf16[640,320]{0,1:T(8,128)(2,1)S(1)}, bf16[640,320]{0,1:T(8,128)(2,1)S(1)}, u32[]{:S(2)}, u32[]{:S(2)}) collective-permute-start(bf16[640,320]{0,1:T(8,128)(2,1)S(1)} %add_convert_fusion.11), channel_id=1, source_target_pairs={{4,0},{8,12},{5,1},{9,13},{6,2},{10,14},{7,3},{11,15},{20,16},{24,... | collective-permute-start | bytes 1228808 | tf_op jit(solution)/shard_map/ppermute | solution.py:760
  682.9 25.9 %collective-permute-start.104 = (bf16[640,320]{0,1:T(8,128)(2,1)S(1)}, bf16[640,320]{0,1:T(8,128)(2,1)S(1)}, u32[]{:S(2)}, u32[]{:S(2)}) collective-permute-start(bf16[640,320]{0,1:T(8,128)(2,1)S(1)} %add_convert_fusion.9), channel_id=1, source_target_pairs={{4,0},{8,12},{5,1},{9,13},{6,2},{10,14},{7,3},{11,15},{20,16},{24,... | collective-permute-start | bytes 1228808 | tf_op jit(solution)/shard_map/ppermute | solution.py:760
  (185 other events, 1869.9 us)
where the time goes:
time: 720 us; the launch traced here: 710 us
  waiting for transfers between devices  265 us (37%)
  starting transfers between devices  161 us (22%)
  Pallas kernels  141 us (20%)
  other arithmetic  58.1 us (8%)
  matrix products  44.4 us (6%)
  local copies, waits for them, and re-layouts  38.2 us (5%)
    ppermute x24, waiting for transfers between devices, hop(): return [lax.ppermute(v, 'ctx', hops[stage]) for v in values]  96.3 us
    ppermute x26, waiting for transfers between devices, blocks(): return lax.ppermute(value, 'ctx', [(i, i ^ slot) for i in range(4)])  72.3 us
    ppermute x24, starting transfers between devices, hop(): return [lax.ppermute(v, 'ctx', hops[stage]) for v in values]  60 us
    ppermute x26, starting transfers between devices, blocks(): return lax.ppermute(value, 'ctx', [(i, i ^ slot) for i in range(4)])  59.2 us
    ppermute x13, waiting for transfers between devices, mate(): return lax.ppermute(value, 'shard', [(0, 1), (1, 0)])  55.5 us
    dot_general x24, matrix products, dot_tn(): return lax.dot_general(left, right, TN, preferred_element_type=F32)  44.4 us
    ppermute x17, waiting for transfers between devices, across(): return lax.ppermute(value, 'tp', [(i, i ^ 2) for i in range(4)])  38.5 us
    pallas_call x2, Pallas kernels, feed(): pl.pallas_call(feed_kernel, grid=(hidden // block,), out_shape=(sds((rows...  32.3 us
  transfers between devices with their start and end apart: 113, of which 37 were waited for; matrix products, arithmetic and copies ran while one was open for 18% of the time, Pallas kernels for 19%

commit v1 on v0

--- a/solution.py
+++ b/solution.py
@@ -678,12 +678,18 @@
     def cut_own(array, m):
         return turn(lax.dynamic_slice_in_dim(array[m], order[0] * quarter, quarter, 0))
 
-    def reduce_rows(parts):
+    def reduce_near(parts):
         keep_a, keep_b, send_a, send_b = parts
         near_b = core(send_b)
         near_a = core(send_a)
-        far = across((keep_b + near_b.astype(F32)).astype(BF))
-        return keep_a, near_a, far
+        return keep_a, near_a, (keep_b + near_b.astype(F32)).astype(BF)
+
+    def reduce_far(found):
+        keep_a, near_a, middle = found
+        return keep_a, near_a, across(middle)
+
+    def reduce_rows(parts):
+        return reduce_far(reduce_near(parts))
 
     def spread_rows(own):
         far = across(own)
@@ -714,29 +720,46 @@
             -1,
         )
         s.plan = jnp.concatenate([jnp.sum(live)[None], listed]).astype(jnp.int32)
-    for m in range(micros):
-        s = state[m]
-        slabs = project(ids, s.normed, qkv, query_shift, value_shift)
+    every = lambda name: [getattr(s, name) for s in state]
+    last = state[-1]
+
+    def tied(values, *others):
+        return list(lax.optimization_barrier((tuple(values),) + others)[0])
+
+    for s, value in zip(state, tied(every("normed"))):
+        s.normed = value
+    previous = ()
+    for m in range(micros):
+        s = state[m]
+        normed = tie(s.normed, *previous)
+        slabs = project(ids, normed, qkv, query_shift, value_shift)
+        previous = (slabs[0],)
         s.slabs = exchange(slabs)
     for m in range(micros):
         s = state[m]
-        found = attend(s.plan, s.slabs, s.mask)
+        found = attend(s.plan, tied(s.slabs, *previous), s.mask)
+        previous = (found[0],)
         s.kept, s.total = found[4:]
         s.heads = exchange(found[:4])
     for m in range(micros):
         s = state[m]
-        s.mixed, *parts = output_part(ids, s.heads, held["o"])
+        s.mixed, *parts = output_part(ids, tied(s.heads, *previous), held["o"])
+        previous = (s.mixed,)
         s.middle, low_two = middle_norm(
             *reduce_rows(parts), s.own, output_shift, gain_two, bias_two
         )
         s.spread = spread_rows(low_two)
-    for m in range(micros):
-        s = state[m]
-        found = feed(s.spread, s.low, held["i"], held["f"], inner_shift)
+    previous = ()
+    for m in range(micros):
+        s = state[m]
+        parts = tied(s.spread, *previous)
+        found = feed(parts, s.low, held["i"], held["f"], inner_shift)
         s.normed_two, s.active, s.inner, s.inner_sum = found[:4]
         s.forward = found[4:8]
         s.final_own = s.low[:quarter]
-        s.keep_two = reduce_rows(found[8:])
+        near = reduce_near(found[8:])
+        previous = (near[2],)
+        s.keep_two = reduce_far(near)
 
     def weight_grad(lefts, rights):
         if paired:
@@ -745,12 +768,12 @@
             home = sum(dot_tn(a[:, :half], b) for a, b in zip(lefts, rights))
             return home, came
         full = sum(dot_tn(a, b) for a, b in zip(lefts, rights))
-        return lax.psum_scatter(
-            full.astype(BF), "shard", scatter_dimension=0, tiled=True
-        ), None
+        return (
+            lax.psum_scatter(full.astype(BF), "shard", scatter_dimension=0, tiled=True),
+        )
 
     def joined(pair):
-        home, came = pair
+        home, came = pair if len(pair) == 2 else (pair[0], None)
         return home if came is None else (home + came.astype(F32)).astype(BF)
 
     inner_pair = (ctx_at == 1) | (ctx_at == 2)
@@ -770,46 +793,47 @@
         step = value.shape[0] // count
         return [value[i * step : (i + 1) * step] for i in range(count)]
 
-    def tied(values, *others):
-        return list(lax.optimization_barrier((tuple(values),) + others)[0])
-
     grads = {}
     pieces = 2 if (width // shard_count) % 32 == 0 else 1
-    every = lambda name: [getattr(s, name) for s in state]
-    outer = weight_grad(every("low"), every("active"))
-    inner = weight_grad(every("normed_two"), every("inner"))
-    for m in range(micros):
-        s = state[m]
-        found = middle_back(*s.keep_two, s.middle, s.final_own, gain_two)
+    previous = ()
+    for m in range(micros):
+        s = state[m]
+        found = middle_back(
+            *tied(s.keep_two, *previous), s.middle, s.final_own, gain_two
+        )
         s.grad_middle, low_middle, s.gain_two, s.bias_two, s.shift_out = found
+        previous = (low_middle,)
         s.low_parts = spread_rows(low_middle)
-    outer = cut(joined(outer), pieces)
-    outer_first = hop(0, outer)
-    for m in range(micros):
-        s = state[m]
-        parts = s.low_parts if m else tied(s.low_parts, outer)
-        s.low_middle, *slabs = attended_grad(ids, parts, held["o"])
+        if m == 0:
+            outer = weight_grad(every("low"), every("active"))
+            inner = weight_grad(every("normed_two"), every("inner"))
+    previous = ()
+    for m in range(micros):
+        s = state[m]
+        s.low_middle, *slabs = attended_grad(ids, tied(s.low_parts, *previous), held["o"])
+        previous = (slabs[0],)
         s.head_grads = exchange(slabs)
     output = weight_grad(every("low_middle"), every("mixed"))
     for m in range(micros):
         s = state[m]
         s.slabs_back = attend_back(
-            s.plan, s.slabs, s.head_grads, s.kept, s.total, s.mask
+            s.plan, s.slabs, tied(s.head_grads, *previous), s.kept, s.total, s.mask
         )
+        previous = (s.slabs_back[0],)
         s.back = exchange(s.slabs_back)
-    inner = cut(joined(inner), pieces)
-    output = [joined(output)]
-    outer = plus(outer, outer_first)
+    outer = cut(joined(tied(outer, *previous)), pieces)
+    outer_first = hop(0, outer)
+    inner = cut(joined(tied(inner, *outer)), pieces)
     inner_first = hop(0, inner)
-    outer_second = hop(1, outer)
+    output = [joined(tied(output, *inner))]
     output_first = hop(0, output)
-    last = micros - 1
-    for m in range(micros):
-        s = state[m]
-        back = s.back if m != last else tied(s.back, inner, outer, output)
-        found = project_back(ids, back, qkv)
+    previous = ()
+    for m in range(micros):
+        s = state[m]
+        found = project_back(ids, tied(s.back, *previous), qkv)
         s.gq, s.gk, s.gv, s.q_sum, s.v_sum = found[:5]
-        s.keep_one = reduce_rows(found[5:])
+        previous = (s.gq,)
+        s.parts_one = found[5:]
     names = "kvq"
     three = {
         n: weight_grad(every("normed"), every(g)) for n, g in zip(names, ("gk", "gv", "gq"))
@@ -817,38 +841,43 @@
     for m in range(micros):
         s = state[m]
         out, s.gain_one, s.bias_one = first_back(
-            *s.keep_one, s.own, s.grad_middle, gain_one
+            *reduce_rows(s.parts_one), s.own, s.grad_middle, gain_one
         )
         s.frames_grad = spread_rows(out)
-    outer = plus(outer, outer_second)
-    inner = plus(inner, inner_first)
-    output = plus(output, output_first)
+    outer = plus(outer, outer_first)
+    outer_second = hop(1, outer)
+    three = {n: [joined(tied(three[n], *outer))] for n in names}
+    three_first = {n: hop(0, three[n]) for n in names}
+    gate = [three[n][0] for n in names]
+    inner = plus(inner, tied(inner_first, *gate))
+    inner_second = hop(1, inner)
+    output = plus(output, tied(output_first, *gate))
+    output_second = hop(1, output)
+    outer = plus(outer, tied(outer_second, *inner))
     outer_third = hop(2, outer)
-    inner_second = hop(1, inner)
-    output_second = hop(1, output)
-    three = {n: tied([joined(three[n])], inner, outer, output) for n in names}
-    three_first = {n: hop(0, three[n]) for n in names}
-    inner = plus(inner, inner_second)
-    output = plus(output, output_second)
+    three = {n: plus(three[n], tied(three_first[n], *outer)) for n in names}
+    three_second = {n: hop(1, three[n]) for n in names}
+    gate = [three[n][0] for n in names]
+    inner = plus(inner, tied(inner_second, *gate))
     inner_third = hop(2, inner)
+    output = plus(output, tied(output_second, *gate))
     output_third = hop(2, output)
-    three = {n: plus(three[n], three_first[n]) for n in names}
-    three_second = {n: hop(1, three[n]) for n in names}
-    three = {n: plus(three[n], three_second[n]) for n in names}
-    for n in names:
-        grads[n] = finish(three[n], hop(2, three[n]))
-    grads["f"] = finish(outer, outer_third)
-    grads["i"] = finish(inner, inner_third)
-    grads["o"] = finish(output, output_third)
-    for m in range(micros):
-        s = state[m]
-        keep, near, far = reduce_rows(tied(s.forward, state[last].slabs_back[0]))
+    three = {n: plus(three[n], tied(three_second[n], *inner)) for n in names}
+    three_third = {n: hop(2, three[n]) for n in names}
+    for m in range(micros):
+        s = state[m]
+        keep, near, far = reduce_rows(tied(s.forward, last.slabs_back[0]))
         final = (
             s.middle + (keep + near.astype(F32) + far.astype(F32)) + outer_shift
         ).astype(BF)
         s.result = spread_rows(final)
     result = gather_rows(ids, sum((s.result for s in state), ()))
     frames_grad = gather_rows(ids, sum((s.frames_grad for s in state), ()))
+    grads["f"] = finish(outer, outer_third)
+    grads["i"] = finish(inner, inner_third)
+    grads["o"] = finish(output, output_third)
+    for n in names:
+        grads[n] = finish(three[n], three_third[n])
 
     def over_all(value):
         value = value + core(value)

time: 720 us -> 700 us (0.972)
  starting transfers between devices: 161 us -> 136 us
  waiting for transfers between devices: 265 us -> 283 us
    ppermute x24, waiting for transfers between devices: 96.3 us -> 144 us  [hop(): return [lax.ppermute(v, 'ctx', hops[stage]) for v in values]]
    ppermute x26, waiting for transfers between devices: 72.3 us -> 38.4 us  [blocks(): return lax.ppermute(value, 'ctx', [(i, i ^ slot) for i in range(4)])]
    ppermute x24, starting transfers between devices: 60 us -> 39.4 us  [hop(): return [lax.ppermute(v, 'ctx', hops[stage]) for v in values]]
    ppermute x13, waiting for transfers between devices: 55.5 us -> 64.5 us  [mate(): return lax.ppermute(value, 'shard', [(0, 1), (1, 0)])]
    convert_element_type x8 -> x13, other arithmetic: 8.16 us -> 16.5 us  [the longest x8 9.85 us: reduce_near(): return (keep_a, near_a, (keep_b + near_b.astype(F32)).astype(BF))]
    unnamed x244 -> x240, local copies, waits for them, and re-layouts: 19.6 us -> 15.1 us
  transfers between devices with their start and end apart: 113 -> 113, of which waited for: 37 -> 28; matrix products, arithmetic and copies ran while one was open for 18% -> 17% of each run, Pallas kernels for 19% -> 19%
where the time goes in v1:
time: 700 us; the launch traced here: 690 us
  waiting for transfers between devices  283 us (40%)
  Pallas kernels  141 us (20%)
  starting transfers between devices  136 us (19%)
  other arithmetic  53 us (8%)
  matrix products  40.8 us (6%)
  local copies, waits for them, and re-layouts  32.4 us (5%)
    ppermute x24, waiting for transfers between devices, hop(): return [lax.ppermute(v, 'ctx', hops[stage]) for v in values]  144 us
    ppermute x13, waiting for transfers between devices, mate(): return lax.ppermute(value, 'shard', [(0, 1), (1, 0)])  64.5 us
    ppermute x26, starting transfers between devices, blocks(): return lax.ppermute(value, 'ctx', [(i, i ^ slot) for i in range(4)])  53.6 us
    dot_general x24, matrix products, dot_tn(): return lax.dot_general(left, right, TN, preferred_element_type=F32)  40.8 us
    ppermute x24, starting transfers between devices, hop(): return [lax.ppermute(v, 'ctx', hops[stage]) for v in values]  39.4 us
    ppermute x26, waiting for transfers between devices, blocks(): return lax.ppermute(value, 'ctx', [(i, i ^ slot) for i in range(4)])  38.4 us
    ppermute x17, waiting for transfers between devices, across(): return lax.ppermute(value, 'tp', [(i, i ^ 2) for i in range(4)])  35.9 us
    pallas_call x2, Pallas kernels, feed(): pl.pallas_call(feed_kernel, grid=(hidden // block,), out_shape=(sds((rows...  32.2 us
  transfers between devices with their start and end apart: 113, of which 28 were waited for; matrix products, arithmetic and copies ran while one was open for 17% of the time, Pallas kernels for 19%

profile of v1, /device:TPU:0, one launch (start us, length us, event | category | flops | bytes accessed | tf_op | source)
XLA Modules:
  0.0 690.3 jit_solution(9166669830450198914)
XLA Ops:
  2.0 3.0 collective-permute-start
  13.9 5.4 shard_map.305
  19.3 5.5 shard_map.306
  37.4 5.7 shard_map.307
  50.2 5.7 shard_map.308
  56.4 3.8 collective-permute-start.5
  62.3 3.7 collective-permute-start.11
  70.1 5.2 collective-permute-done.5.x3
  78.6 13.0 %collective-permute-start.6 = (bf16[80,512]{1,0:T(8,128)(2,1)}, bf16[80,512]{1,0:T(8,128)(2,1)S(1)}, u32[]{:S(2)}, u32[]{:S(2)}) collective-permute-start(bf16[80,512]{1,0:T(8,128)(2,1)} %get-tuple-element.240), channel_id=1, source_target_pairs={{0,4},{4,0},{8,12},{12,8},{1,5},{5,1},{9,13},{13,9},{2,6},{6,2},{1... | collective-permute-start | bytes 245768 | tf_op jit(solution)/shard_map/ppermute | solution.py:623
  96.3 10.1 %shard_map.310 = (bf16[80,512]{1,0:T(8,128)(2,1)}, bf16[80,512]{1,0:T(8,128)(2,1)}, bf16[80,512]{1,0:T(8,128)(2,1)}, bf16[80,512]{1,0:T(8,128)(2,1)}, f32[4,80,512]{2,1,0:T(8,128)}, /*index=5*/f32[4,1,512]{2,1,0:T(1,128)}) custom-call(s32[5]{0:T(128)} %pad_add_fusion.4.plan, bf16[240,512]{1,0:T(8,128)(2,1)} %get-tuple-element.246.x0, ...), custom_call_target="tpu_custom_call" | custom-call | tf_op jit(solution)/shard_map/pallas_call | solution.py:172
  107.8 3.6 shard_map.311
  116.6 3.4 collective-permute-start.19
  123.8 3.7 shard_map.314
  132.5 6.2 collective-permute-done.15.second
  145.8 7.0 %collective-permute-done.16.n1 = bf16[128,1280]{1,0:T(8,128)(2,1)} collective-permute-done((bf16[128,1280]{1,0:T(8,128)(2,1)}, bf16[128,1280]{1,0:T(8,128)(2,1)}, u32[]{:S(2)}, u32[]{:S(2)}) %collective-permute-start.16) | collective-permute-done | bytes 327712 | tf_op jit(solution)/shard_map/ppermute | solution.py:620
  162.3 28.7 %collective-permute-done.20.ob = bf16[640,1280]{1,0:T(8,128)(2,1)} collective-permute-done((bf16[640,1280]{1,0:T(8,128)(2,1)}, bf16[640,1280]{1,0:T(8,128)(2,1)}, u32[]{:S(2)}, u32[]{:S(2)}) %collective-permute-start.20) | collective-permute-done | bytes 1638432 | tf_op jit(solution)/shard_map/ppermute | solution.py:626
  191.1 15.9 %shard_map.313 = (bf16[512,1280]{1,0:T(8,128)(2,1)}, bf16[512,1280]{1,0:T(8,128)(2,1)}, bf16[512,1280]{1,0:T(8,128)(2,1)}, f32[1,1280]{1,0:T(1,128)}, f32[128,12...) custom-call(bf16[128,1280]{1,0:T(8,128)(2,1)} %get-tuple-element.262, ...), custom_call_target="tpu_custom_call" | custom-call | tf_op jit(solution)/shard_map/pallas_call | solution.py:408
  213.7 16.3 %shard_map.316 = (bf16[512,1280]{1,0:T(8,128)(2,1)}, bf16[512,1280]{1,0:T(8,128)(2,1)}, bf16[512,1280]{1,0:T(8,128)(2,1)}, f32[1,1280]{1,0:T(1,128)}, f32[128,12...) custom-call(bf16[128,1280]{1,0:T(8,128)(2,1)} %get-tuple-element.288, ...), custom_call_target="tpu_custom_call" | custom-call | tf_op jit(solution)/shard_map/pallas_call | solution.py:408
  247.7 3.1 shard_map.317
  252.4 3.4 collective-permute-done.33.second
  255.7 3.2 shard_map.318
  262.8 6.0 collective-permute-done.36.l1
  269.4 3.4 shard_map.319
  272.7 3.0 collective-permute-start.46
  277.1 3.5 shard_map.320
  284.7 3.0 collective-permute-start.43
  289.7 3.7 shard_map.321
  293.4 3.0 collective-permute-start.61
  300.7 15.9 %shard_map.322 = (bf16[240,512]{1,0:T(8,128)(2,1)}, bf16[240,512]{1,0:T(8,128)(2,1)}, bf16[240,512]{1,0:T(8,128)(2,1)}, bf16[240,512]{1,0:T(8,128)(2,1)}) custom-call(s32[5]{0:T(128)} %pad_add_fusion.4.plan, bf16[240,512]{1,0:T(8,128)(2,1)} %get-tuple-element.246.x0, bf16[240,512]{1,0:T(8,128)(2,1)} %copy-done.43, bf16[240,512]{1,0:T(8,128)(2,1)} %copy-done.44, ...), custom_call_target="tpu_custom_call" | custom-call | tf_op jit(solution)/shard_map/pallas_call | solution.py:264
  316.6 3.0 collective-permute-start.70
  325.8 6.0 shard_map.324
  331.8 5.1 collective-permute-done.70.s2
  336.9 6.0 shard_map.326
  370.2 24.6 %collective-permute-done.90 = bf16[640,1280]{1,0:T(8,128)(2,1)} collective-permute-done((bf16[640,1280]{1,0:T(8,128)(2,1)}, bf16[640,1280]{1,0:T(8,128)(2,1)}, u32[]{:S(2)}, u32[]{:S(2)}) %collective-permute-start.90) | collective-permute-done | bytes 1638432 | tf_op jit(solution)/shard_map/ppermute | solution.py:626
  399.4 2.9 shard_map.327
  414.4 7.8 %collective-permute-done.80 = f32[8,1280]{1,0:T(8,128)S(1)} collective-permute-done((f32[8,1280]{1,0:T(8,128)S(1)}, f32[8,1280]{1,0:T(8,128)S(1)}, u32[]{:S(2)}, u32[]{:S(2)}) %collective-permute-start.80) | collective-permute-done | bytes 40992 | tf_op jit(solution)/shard_map/ppermute | solution.py:626
  432.0 27.2 %collective-permute-done.81 = f32[8,1280]{1,0:T(8,128)S(1)} collective-permute-done((f32[8,1280]{1,0:T(8,128)S(1)}, f32[8,1280]{1,0:T(8,128)S(1)}, u32[]{:S(2)}, u32[]{:S(2)}) %collective-permute-start.81) | collective-permute-done | bytes 40992 | tf_op jit(solution)/shard_map/ppermute | solution.py:623
  459.1 4.4 collective-permute-start.91
  469.8 35.6 %collective-permute-done.106 = bf16[640,320]{0,1:T(8,128)(2,1)S(1)} collective-permute-done((bf16[640,320]{0,1:T(8,128)(2,1)S(1)}, bf16[640,320]{0,1:T(8,128)(2,1)S(1)}, u32[]{:S(2)}, u32[]{:S(2)}) %collective-permute-start.106) | collective-permute-done | bytes 409632 | tf_op jit(solution)/shard_map/ppermute | solution.py:783
  508.8 3.4 collective-permute-start.82
  517.8 4.0 collective-permute-done.66.refs_1_
  528.5 5.7 shard_map.323
  534.2 7.7 %collective-permute-start.87 = (bf16[640,320]{0,1:T(8,128)(2,1)}, bf16[640,320]{0,1:T(8,128)(2,1)}, u32[]{:S(2)}, u32[]{:S(2)}) collective-permute-start(bf16[640,320]{0,1:T(8,128)(2,1)} %add_convert_fusion.21), channel_id=1, source_target_pairs={{0,4},{12,8},{1,5},{13,9},{2,6},{14,10},{3,7},{15,11},{16,20},{28,... | collective-permute-start | bytes 1228808 | tf_op jit(solution)/shard_map/ppermute | solution.py:783
  546.0 5.7 shard_map.328
  556.8 3.3 collective-permute-done.98
  562.5 5.8 collective-permute-done.99
  578.8 89.7 %collective-permute-done.108 = bf16[640,320]{0,1:T(8,128)(2,1)S(1)} collective-permute-done((bf16[640,320]{0,1:T(8,128)(2,1)S(1)}, bf16[640,320]{0,1:T(8,128)(2,1)S(1)}, u32[]{:S(2)}, u32[]{:S(2)}) %collective-permute-start.108) | collective-permute-done | bytes 409632 | tf_op jit(solution)/shard_map/ppermute | solution.py:783
  673.7 6.4 collective-permute-done.100
  (596 shorter events, 235.8 us)
Async XLA Ops:
  2.0 33.1 %collective-permute-start = (bf16[640,320]{1,0:T(8,128)(2,1)S(1)}, bf16[640,320]{1,0:T(8,128)(2,1)}, u32[]{:S(2)}, u32[]{:S(2)}) collective-permute-start(bf16[640,320]{1,0:T(8,128)(2,1)S(1)} %copy.58.qa), channel_id=1, source_target_pairs={{0,16},{16,0},{1,17},{17,1},{2,18},{18,2},{3,19},{19,3},{4,20},{20... | collective-permute-start | bytes 1228808 | tf_op jit(solution)/shard_map/ppermute | solution.py:626
  7.0 28.1 %collective-permute-start.1 = (bf16[640,320]{1,0:T(8,128)(2,1)}, bf16[640,320]{1,0:T(8,128)(2,1)}, u32[]{:S(2)}, u32[]{:S(2)}) collective-permute-start(bf16[640,320]{1,0:T(8,128)(2,1)} %copy.59.ka), channel_id=1, source_target_pairs={{0,16},{16,0},{1,17},{17,1},{2,18},{18,2},{3,19},{19,3},{4,20},{20... | collective-permute-start | bytes 1228808 | tf_op jit(solution)/shard_map/ppermute | solution.py:626
  8.2 29.3 %collective-permute-start.2 = (bf16[640,320]{1,0:T(8,128)(2,1)}, bf16[640,320]{1,0:T(8,128)(2,1)}, u32[]{:S(2)}, u32[]{:S(2)}) collective-permute-start(bf16[640,320]{1,0:T(8,128)(2,1)} %copy.60.va), channel_id=1, source_target_pairs={{0,16},{16,0},{1,17},{17,1},{2,18},{18,2},{3,19},{19,3},{4,20},{20... | collective-permute-start | bytes 1228808 | tf_op jit(solution)/shard_map/ppermute | solution.py:626
  55.9 35.7 %collective-permute-start.9 = (bf16[240,512]{1,0:T(8,128)(2,1)}, bf16[240,512]{1,0:T(8,128)(2,1)S(1)}, u32[]{:S(2)}, u32[]{:S(2)}) collective-permute-start(bf16[240,512]{1,0:T(8,128)(2,1)} %get-tuple-element.243), channel_id=1, source_target_pairs={{0,4},{4,0},{8,12},{12,8},{1,5},{5,1},{9,13},{13,9},{2,6},{6,2},{1... | collective-permute-start | bytes 737288 | tf_op jit(solution)/shard_map/ppermute | solution.py:623
  56.4 36.5 %collective-permute-start.10 = (bf16[240,512]{1,0:T(8,128)(2,1)}, bf16[240,512]{1,0:T(8,128)(2,1)S(1)}, u32[]{:S(2)}, u32[]{:S(2)}) collective-permute-start(bf16[240,512]{1,0:T(8,128)(2,1)} %get-tuple-element.244), channel_id=1, source_target_pairs={{0,8},{4,12},{8,0},{12,4},{1,9},{5,13},{9,1},{13,5},{2,10},{6,14},... | collective-permute-start | bytes 737288 | tf_op jit(solution)/shard_map/ppermute | solution.py:623
  56.4 18.9 %collective-permute-start.5 = (bf16[240,512]{1,0:T(8,128)(2,1)}, bf16[240,512]{1,0:T(8,128)(2,1)S(1)}, u32[]{:S(2)}, u32[]{:S(2)}) collective-permute-start(bf16[240,512]{1,0:T(8,128)(2,1)} %get-tuple-element.231), channel_id=1, source_target_pairs={{0,12},{4,8},{8,4},{12,0},{1,13},{5,9},{9,5},{13,1},{2,14},{6,10},... | collective-permute-start | bytes 737288 | tf_op jit(solution)/shard_map/ppermute | solution.py:623
  60.6 45.8 %collective-permute-start.12 = (bf16[640,320]{1,0:T(8,128)(2,1)S(1)}, bf16[640,320]{1,0:T(8,128)(2,1)S(1)}, u32[]{:S(2)}, u32[]{:S(2)}) collective-permute-start(bf16[640,320]{1,0:T(8,128)(2,1)S(1)} %copy.64), channel_id=1, source_target_pairs={{0,16},{16,0},{1,17},{17,1},{2,18},{18,2},{3,19},{19,3},{4,20},{20... | collective-permute-start | bytes 1228808 | tf_op jit(solution)/shard_map/ppermute | solution.py:626
  62.3 33.3 %collective-permute-start.11 = (bf16[240,512]{1,0:T(8,128)(2,1)}, bf16[240,512]{1,0:T(8,128)(2,1)S(1)}, u32[]{:S(2)}, u32[]{:S(2)}) collective-permute-start(bf16[240,512]{1,0:T(8,128)(2,1)} %get-tuple-element.245), channel_id=1, source_target_pairs={{0,12},{4,8},{8,4},{12,0},{1,13},{5,9},{9,5},{13,1},{2,14},{6,10},... | collective-permute-start | bytes 737288 | tf_op jit(solution)/shard_map/ppermute | solution.py:623
  78.6 27.7 %collective-permute-start.6 = (bf16[80,512]{1,0:T(8,128)(2,1)}, bf16[80,512]{1,0:T(8,128)(2,1)S(1)}, u32[]{:S(2)}, u32[]{:S(2)}) collective-permute-start(bf16[80,512]{1,0:T(8,128)(2,1)} %get-tuple-element.240), channel_id=1, source_target_pairs={{0,4},{4,0},{8,12},{12,8},{1,5},{5,1},{9,13},{13,9},{2,6},{6,2},{1... | collective-permute-start | bytes 245768 | tf_op jit(solution)/shard_map/ppermute | solution.py:623
  116.6 45.7 %collective-permute-start.19 = (bf16[640,1280]{1,0:T(8,128)(2,1)}, bf16[640,1280]{1,0:T(8,128)(2,1)}, u32[]{:S(2)}, u32[]{:S(2)}) collective-permute-start(bf16[640,1280]{1,0:T(8,128)(2,1)} %ia.3), channel_id=1, source_target_pairs={{0,16},{16,0},{1,17},{17,1},{2,18},{18,2},{3,19},{19,3},{4,20},{20... | collective-permute-start | bytes 4915208 | tf_op jit(solution)/shard_map/ppermute | solution.py:626
  120.0 71.1 %collective-permute-start.20 = (bf16[640,1280]{1,0:T(8,128)(2,1)}, bf16[640,1280]{1,0:T(8,128)(2,1)}, u32[]{:S(2)}, u32[]{:S(2)}) collective-permute-start(bf16[640,1280]{1,0:T(8,128)(2,1)} %oa.3), channel_id=1, source_target_pairs={{0,16},{16,0},{1,17},{17,1},{2,18},{18,2},{3,19},{19,3},{4,20},{20... | collective-permute-start | bytes 4915208 | tf_op jit(solution)/shard_map/ppermute | solution.py:626
  160.8 46.9 %collective-permute-start.27 = (bf16[128,1280]{1,0:T(8,128)(2,1)}, bf16[128,1280]{1,0:T(8,128)(2,1)S(1)}, u32[]{:S(2)}, u32[]{:S(2)}) collective-permute-start(bf16[128,1280]{1,0:T(8,128)(2,1)} %get-tuple-element.288.n0), channel_id=1, source_target_pairs={{0,2},{1,3},{2,0},{3,1},{4,6},{5,7},{6,4},{7,5},{8,10},{9,11},{10,... | collective-permute-start | bytes 983048 | tf_op jit(solution)/shard_map/ppermute | solution.py:620
  207.8 39.9 %collective-permute-start.34 = (bf16[128,1280]{1,0:T(8,128)(2,1)}, bf16[128,1280]{1,0:T(8,128)(2,1)}, u32[]{:S(2)}, u32[]{:S(2)}) collective-permute-start(bf16[128,1280]{1,0:T(8,128)(2,1)} %get-tuple-element.298), channel_id=1, source_target_pairs={{0,1},{1,0},{2,3},{3,2},{4,5},{5,4},{6,7},{7,6},{8,9},{9,8},{10,11... | collective-permute-start | bytes 983048 | tf_op jit(solution)/shard_map/ppermute | solution.py:617
  210.7 36.9 %collective-permute-start.35 = (bf16[128,1280]{1,0:T(8,128)(2,1)}, bf16[128,1280]{1,0:T(8,128)(2,1)}, u32[]{:S(2)}, u32[]{:S(2)}) collective-permute-start(bf16[128,1280]{1,0:T(8,128)(2,1)} %add_convert_fusion.29), channel_id=1, source_target_pairs={{0,2},{1,3},{2,0},{3,1},{4,6},{5,7},{6,4},{7,5},{8,10},{9,11},{10,... | collective-permute-start | bytes 983048 | tf_op jit(solution)/shard_map/ppermute | solution.py:620
  293.4 26.2 %collective-permute-start.60 = (bf16[240,512]{1,0:T(8,128)(2,1)}, bf16[240,512]{1,0:T(8,128)(2,1)S(1)}, u32[]{:S(2)}, u32[]{:S(2)}) collective-permute-start(bf16[240,512]{1,0:T(8,128)(2,1)} %get-tuple-element.350), channel_id=1, source_target_pairs={{0,4},{4,0},{8,12},{12,8},{1,5},{5,1},{9,13},{13,9},{2,6},{6,2},{1... | collective-permute-start | bytes 737288 | tf_op jit(solution)/shard_map/ppermute | solution.py:623
  293.4 30.3 %collective-permute-start.61 = (bf16[240,512]{1,0:T(8,128)(2,1)}, bf16[240,512]{1,0:T(8,128)(2,1)}, u32[]{:S(2)}, u32[]{:S(2)}) collective-permute-start(bf16[240,512]{1,0:T(8,128)(2,1)} %get-tuple-element.351), channel_id=1, source_target_pairs={{0,8},{4,12},{8,0},{12,4},{1,9},{5,13},{9,1},{13,5},{2,10},{6,14},... | collective-permute-start | bytes 737288 | tf_op jit(solution)/shard_map/ppermute | solution.py:623
  299.3 24.4 %collective-permute-start.62 = (bf16[240,512]{1,0:T(8,128)(2,1)}, bf16[240,512]{1,0:T(8,128)(2,1)}, u32[]{:S(2)}, u32[]{:S(2)}) collective-permute-start(bf16[240,512]{1,0:T(8,128)(2,1)} %get-tuple-element.352), channel_id=1, source_target_pairs={{0,12},{4,8},{8,4},{12,0},{1,13},{5,9},{9,5},{13,1},{2,14},{6,10},... | collective-permute-start | bytes 737288 | tf_op jit(solution)/shard_map/ppermute | solution.py:623
  316.6 20.3 %collective-permute-start.70 = (bf16[240,512]{1,0:T(8,128)(2,1)}, bf16[240,512]{1,0:T(8,128)(2,1)}, u32[]{:S(2)}, u32[]{:S(2)}) collective-permute-start(bf16[240,512]{1,0:T(8,128)(2,1)} %get-tuple-element.364), channel_id=1, source_target_pairs={{0,8},{4,12},{8,0},{12,4},{1,9},{5,13},{9,1},{13,5},{2,10},{6,14},... | collective-permute-start | bytes 737288 | tf_op jit(solution)/shard_map/ppermute | solution.py:623
  323.7 39.0 %collective-permute-start.84 = (bf16[640,1280]{1,0:T(8,128)(2,1)}, bf16[640,1280]{1,0:T(8,128)(2,1)}, u32[]{:S(2)}, u32[]{:S(2)}) collective-permute-start(bf16[640,1280]{1,0:T(8,128)(2,1)} %fusion), channel_id=1, source_target_pairs={{0,16},{16,0},{1,17},{17,1},{2,18},{18,2},{3,19},{19,3},{4,20},{20... | collective-permute-start | bytes 4915208 | tf_op jit(solution)/shard_map/ppermute | solution.py:626
  323.8 71.1 %collective-permute-start.90 = (bf16[640,1280]{1,0:T(8,128)(2,1)}, bf16[640,1280]{1,0:T(8,128)(2,1)}, u32[]{:S(2)}, u32[]{:S(2)}) collective-permute-start(bf16[640,1280]{1,0:T(8,128)(2,1)} %fusion.1), channel_id=1, source_target_pairs={{0,16},{16,0},{1,17},{17,1},{2,18},{18,2},{3,19},{19,3},{4,20},{20... | collective-permute-start | bytes 4915208 | tf_op jit(solution)/shard_map/ppermute | solution.py:626
  331.7 63.1 %collective-permute-start.63 = (bf16[128,1280]{1,0:T(8,128)(2,1)}, bf16[128,1280]{1,0:T(8,128)(2,1)}, u32[]{:S(2)}, u32[]{:S(2)}) collective-permute-start(bf16[128,1280]{1,0:T(8,128)(2,1)} %get-tuple-element.358), channel_id=1, source_target_pairs={{0,1},{1,0},{2,3},{3,2},{4,5},{5,4},{6,7},{7,6},{8,9},{9,8},{10,11... | collective-permute-start | bytes 983048 | tf_op jit(solution)/shard_map/ppermute | solution.py:617
  336.9 27.7 %collective-permute-start.64 = (bf16[128,1280]{1,0:T(8,128)(2,1)}, bf16[128,1280]{1,0:T(8,128)(2,1)}, u32[]{:S(2)}, u32[]{:S(2)}) collective-permute-start(bf16[128,1280]{1,0:T(8,128)(2,1)} %get-tuple-element.360), channel_id=1, source_target_pairs={{0,1},{1,0},{2,3},{3,2},{4,5},{5,4},{6,7},{7,6},{8,9},{9,8},{10,11... | collective-permute-start | bytes 983048 | tf_op jit(solution)/shard_map/ppermute | solution.py:617
  349.7 49.6 %collective-permute-start.72 = (bf16[128,1280]{1,0:T(8,128)(2,1)}, bf16[128,1280]{1,0:T(8,128)(2,1)}, u32[]{:S(2)}, u32[]{:S(2)}) collective-permute-start(bf16[128,1280]{1,0:T(8,128)(2,1)} %get-tuple-element.372), channel_id=1, source_target_pairs={{0,1},{1,0},{2,3},{3,2},{4,5},{5,4},{6,7},{7,6},{8,9},{9,8},{10,11... | collective-permute-start | bytes 983048 | tf_op jit(solution)/shard_map/ppermute | solution.py:617
  366.0 29.1 %collective-permute-start.65 = (bf16[128,1280]{1,0:T(8,128)(2,1)S(1)}, bf16[128,1280]{1,0:T(8,128)(2,1)S(1)}, u32[]{:S(2)}, u32[]{:S(2)}) collective-permute-start(bf16[128,1280]{1,0:T(8,128)(2,1)S(1)} %add_convert_fusion.23), channel_id=1, source_target_pairs={{0,2},{1,3},{2,0},{3,1},{4,6},{5,7},{6,4},{7,5},{8,10},{9,11},{10,... | collective-permute-start | bytes 983048 | tf_op jit(solution)/shard_map/ppermute | solution.py:620
  367.4 31.9 %collective-permute-start.74 = (bf16[128,1280]{1,0:T(8,128)(2,1)}, bf16[128,1280]{1,0:T(8,128)(2,1)}, u32[]{:S(2)}, u32[]{:S(2)}) collective-permute-start(bf16[128,1280]{1,0:T(8,128)(2,1)} %add_convert_fusion.22), channel_id=1, source_target_pairs={{0,2},{1,3},{2,0},{3,1},{4,6},{5,7},{6,4},{7,5},{8,10},{9,11},{10,... | collective-permute-start | bytes 983048 | tf_op jit(solution)/shard_map/ppermute | solution.py:620
  394.8 18.9 %collective-permute-start.105 = (bf16[640,320]{0,1:T(8,128)(2,1)}, bf16[640,320]{0,1:T(8,128)(2,1)}, u32[]{:S(2)}, u32[]{:S(2)}) collective-permute-start(bf16[640,320]{0,1:T(8,128)(2,1)} %fusion.5), channel_id=1, source_target_pairs={{0,16},{16,0},{1,17},{17,1},{2,18},{18,2},{3,19},{19,3},{4,20},{20... | collective-permute-start | bytes 1228808 | tf_op jit(solution)/shard_map/ppermute | solution.py:626
  395.8 27.1 %collective-permute-start.54 = (bf16[128,1280]{1,0:T(8,128)(2,1)}, bf16[128,1280]{1,0:T(8,128)(2,1)}, u32[]{:S(2)}, u32[]{:S(2)}) collective-permute-start(bf16[128,1280]{1,0:T(8,128)(2,1)} %get-tuple-element.347), channel_id=1, source_target_pairs={{0,1},{1,0},{2,3},{3,2},{4,5},{5,4},{6,7},{7,6},{8,9},{9,8},{10,11... | collective-permute-start | bytes 983048 | tf_op jit(solution)/shard_map/ppermute | solution.py:617
  422.9 44.8 %collective-permute-start.86 = (bf16[320,1280]{1,0:T(8,128)(2,1)S(1)}, bf16[320,1280]{1,0:T(8,128)(2,1)S(1)}, u32[]{:S(2)}, u32[]{:S(2)}) collective-permute-start(bf16[320,1280]{1,0:T(8,128)(2,1)S(1)} %copy-done.50), channel_id=1, source_target_pairs={{0,4},{12,8},{1,5},{13,9},{2,6},{14,10},{3,7},{15,11},{16,20},{28,... | collective-permute-start | bytes 2457608 | tf_op jit(solution)/shard_map/ppermute | solution.py:783
  424.4 44.9 %collective-permute-start.85 = (bf16[320,1280]{1,0:T(8,128)(2,1)S(1)}, bf16[320,1280]{1,0:T(8,128)(2,1)S(1)}, u32[]{:S(2)}, u32[]{:S(2)}) collective-permute-start(bf16[320,1280]{1,0:T(8,128)(2,1)S(1)} %copy-done.49), channel_id=1, source_target_pairs={{0,4},{12,8},{1,5},{13,9},{2,6},{14,10},{3,7},{15,11},{16,20},{28,... | collective-permute-start | bytes 2457608 | tf_op jit(solution)/shard_map/ppermute | solution.py:783
  425.8 33.3 %collective-permute-start.81 = (f32[8,1280]{1,0:T(8,128)S(1)}, f32[8,1280]{1,0:T(8,128)S(1)}, u32[]{:S(2)}, u32[]{:S(2)}) collective-permute-start(f32[8,1280]{1,0:T(8,128)S(1)} %add.318), channel_id=1, source_target_pairs={{0,4},{4,0},{8,12},{12,8},{1,5},{5,1},{9,13},{13,9},{2,6},{6,2},{1... | collective-permute-start | bytes 122888 | tf_op jit(solution)/shard_map/ppermute | solution.py:623
  427.0 38.0 %collective-permute-start.94 = (bf16[640,320]{0,1:T(8,128)(2,1)S(1)}, bf16[640,320]{0,1:T(8,128)(2,1)S(1)}, u32[]{:S(2)}, u32[]{:S(2)}) collective-permute-start(bf16[640,320]{0,1:T(8,128)(2,1)S(1)} %copy-done.65), channel_id=1, source_target_pairs={{0,16},{16,0},{1,17},{17,1},{2,18},{18,2},{3,19},{19,3},{4,20},{20... | collective-permute-start | bytes 1228808 | tf_op jit(solution)/shard_map/ppermute | solution.py:626
  430.5 35.9 %collective-permute-start.93 = (bf16[640,320]{0,1:T(8,128)(2,1)S(1)}, bf16[640,320]{0,1:T(8,128)(2,1)S(1)}, u32[]{:S(2)}, u32[]{:S(2)}) collective-permute-start(bf16[640,320]{0,1:T(8,128)(2,1)S(1)} %copy-done.64), channel_id=1, source_target_pairs={{0,16},{16,0},{1,17},{17,1},{2,18},{18,2},{3,19},{19,3},{4,20},{20... | collective-permute-start | bytes 1228808 | tf_op jit(solution)/shard_map/ppermute | solution.py:626
  459.1 48.4 %collective-permute-start.91 = (bf16[320,1280]{1,0:T(8,128)(2,1)S(1)}, bf16[320,1280]{1,0:T(8,128)(2,1)S(1)}, u32[]{:S(2)}, u32[]{:S(2)}) collective-permute-start(bf16[320,1280]{1,0:T(8,128)(2,1)S(1)} %get-tuple-element.463), channel_id=1, source_target_pairs={{0,4},{12,8},{1,5},{13,9},{2,6},{14,10},{3,7},{15,11},{16,20},{28,... | collective-permute-start | bytes 2457608 | tf_op jit(solution)/shard_map/ppermute | solution.py:783
  465.1 43.7 %collective-permute-start.92 = (bf16[320,1280]{1,0:T(8,128)(2,1)S(1)}, bf16[320,1280]{1,0:T(8,128)(2,1)S(1)}, u32[]{:S(2)}, u32[]{:S(2)}) collective-permute-start(bf16[320,1280]{1,0:T(8,128)(2,1)S(1)} %get-tuple-element.462), channel_id=1, source_target_pairs={{0,4},{12,8},{1,5},{13,9},{2,6},{14,10},{3,7},{15,11},{16,20},{28,... | collective-permute-start | bytes 2457608 | tf_op jit(solution)/shard_map/ppermute | solution.py:783
  466.4 38.9 %collective-permute-start.106 = (bf16[640,320]{0,1:T(8,128)(2,1)S(1)}, bf16[640,320]{0,1:T(8,128)(2,1)S(1)}, u32[]{:S(2)}, u32[]{:S(2)}) collective-permute-start(bf16[640,320]{0,1:T(8,128)(2,1)S(1)} %add_convert_fusion.12), channel_id=1, source_target_pairs={{0,4},{12,8},{1,5},{13,9},{2,6},{14,10},{3,7},{15,11},{16,20},{28,... | collective-permute-start | bytes 1228808 | tf_op jit(solution)/shard_map/ppermute | solution.py:783
  467.8 39.0 %collective-permute-start.51 = (bf16[128,1280]{1,0:T(8,128)(2,1)S(1)}, bf16[128,1280]{1,0:T(8,128)(2,1)}, u32[]{:S(2)}, u32[]{:S(2)}) collective-permute-start(bf16[128,1280]{1,0:T(8,128)(2,1)S(1)} %get-tuple-element.475.refs_0_), channel_id=1, source_target_pairs={{0,2},{1,3},{2,0},{3,1},{4,6},{5,7},{6,4},{7,5},{8,10},{9,11},{10,... | collective-permute-start | bytes 983048 | tf_op jit(solution)/shard_map/ppermute | solution.py:620
  469.3 37.5 %collective-permute-start.52 = (bf16[128,1280]{1,0:T(8,128)(2,1)S(1)}, bf16[128,1280]{1,0:T(8,128)(2,1)S(1)}, u32[]{:S(2)}, u32[]{:S(2)}) collective-permute-start(bf16[128,1280]{1,0:T(8,128)(2,1)S(1)} %get-tuple-element.475.refs_0_), channel_id=1, source_target_pairs={{0,1},{1,0},{2,3},{3,2},{4,5},{5,4},{6,7},{7,6},{8,9},{9,8},{10,11... | collective-permute-start | bytes 983048 | tf_op jit(solution)/shard_map/ppermute | solution.py:617
  521.9 29.8 %collective-permute-start.88 = (bf16[320,1280]{1,0:T(8,128)(2,1)S(1)}, bf16[320,1280]{1,0:T(8,128)(2,1)}, u32[]{:S(2)}, u32[]{:S(2)}) collective-permute-start(bf16[320,1280]{1,0:T(8,128)(2,1)S(1)} %get-tuple-element.465), channel_id=1, source_target_pairs={{4,8},{8,4},{5,9},{9,5},{6,10},{10,6},{7,11},{11,7},{20,24},{24,20... | collective-permute-start | bytes 2457608 | tf_op jit(solution)/shard_map/ppermute | solution.py:783
  523.4 29.0 %collective-permute-start.89 = (bf16[320,1280]{1,0:T(8,128)(2,1)S(1)}, bf16[320,1280]{1,0:T(8,128)(2,1)}, u32[]{:S(2)}, u32[]{:S(2)}) collective-permute-start(bf16[320,1280]{1,0:T(8,128)(2,1)S(1)} %get-tuple-element.464), channel_id=1, source_target_pairs={{4,8},{8,4},{5,9},{9,5},{6,10},{10,6},{7,11},{11,7},{20,24},{24,20... | collective-permute-start | bytes 2457608 | tf_op jit(solution)/shard_map/ppermute | solution.py:783
  534.2 21.8 %collective-permute-start.87 = (bf16[640,320]{0,1:T(8,128)(2,1)}, bf16[640,320]{0,1:T(8,128)(2,1)}, u32[]{:S(2)}, u32[]{:S(2)}) collective-permute-start(bf16[640,320]{0,1:T(8,128)(2,1)} %add_convert_fusion.21), channel_id=1, source_target_pairs={{0,4},{12,8},{1,5},{13,9},{2,6},{14,10},{3,7},{15,11},{16,20},{28,... | collective-permute-start | bytes 1228808 | tf_op jit(solution)/shard_map/ppermute | solution.py:783
  544.0 24.3 %collective-permute-start.99 = (bf16[640,320]{0,1:T(8,128)(2,1)}, bf16[640,320]{0,1:T(8,128)(2,1)}, u32[]{:S(2)}, u32[]{:S(2)}) collective-permute-start(bf16[640,320]{0,1:T(8,128)(2,1)} %get-tuple-element.502), channel_id=1, source_target_pairs={{0,4},{12,8},{1,5},{13,9},{2,6},{14,10},{3,7},{15,11},{16,20},{28,... | collective-permute-start | bytes 1228808 | tf_op jit(solution)/shard_map/ppermute | solution.py:783
  551.7 19.5 %collective-permute-start.96 = (bf16[320,1280]{1,0:T(8,128)(2,1)S(1)}, bf16[320,1280]{1,0:T(8,128)(2,1)S(1)}, u32[]{:S(2)}, u32[]{:S(2)}) collective-permute-start(bf16[320,1280]{1,0:T(8,128)(2,1)S(1)} %get-tuple-element.461), channel_id=1, source_target_pairs={{4,8},{8,4},{5,9},{9,5},{6,10},{10,6},{7,11},{11,7},{20,24},{24,20... | collective-permute-start | bytes 2457608 | tf_op jit(solution)/shard_map/ppermute | solution.py:783
  552.4 19.5 %collective-permute-start.97 = (bf16[320,1280]{1,0:T(8,128)(2,1)S(1)}, bf16[320,1280]{1,0:T(8,128)(2,1)S(1)}, u32[]{:S(2)}, u32[]{:S(2)}) collective-permute-start(bf16[320,1280]{1,0:T(8,128)(2,1)S(1)} %get-tuple-element.460), channel_id=1, source_target_pairs={{4,8},{8,4},{5,9},{9,5},{6,10},{10,6},{7,11},{11,7},{20,24},{24,20... | collective-permute-start | bytes 2457608 | tf_op jit(solution)/shard_map/ppermute | solution.py:783
  560.1 113.4 %collective-permute-start.112 = (bf16[320,1280]{1,0:T(8,128)(2,1)S(1)}, bf16[320,1280]{1,0:T(8,128)(2,1)S(1)}, u32[]{:S(2)}, u32[]{:S(2)}) collective-permute-start(bf16[320,1280]{1,0:T(8,128)(2,1)S(1)} %add_convert_fusion.4), channel_id=1, source_target_pairs={{4,0},{8,12},{5,1},{9,13},{6,2},{10,14},{7,3},{11,15},{20,16},{24,... | collective-permute-start | bytes 2457608 | tf_op jit(solution)/shard_map/ppermute | solution.py:783
  573.1 97.6 %collective-permute-start.110 = (bf16[320,1280]{1,0:T(8,128)(2,1)S(1)}, bf16[320,1280]{1,0:T(8,128)(2,1)S(1)}, u32[]{:S(2)}, u32[]{:S(2)}) collective-permute-start(bf16[320,1280]{1,0:T(8,128)(2,1)S(1)} %add_convert_fusion.2), channel_id=1, source_target_pairs={{4,0},{8,12},{5,1},{9,13},{6,2},{10,14},{7,3},{11,15},{20,16},{24,... | collective-permute-start | bytes 2457608 | tf_op jit(solution)/shard_map/ppermute | solution.py:783
  574.5 97.6 %collective-permute-start.109 = (bf16[320,1280]{1,0:T(8,128)(2,1)S(1)}, bf16[320,1280]{1,0:T(8,128)(2,1)S(1)}, u32[]{:S(2)}, u32[]{:S(2)}) collective-permute-start(bf16[320,1280]{1,0:T(8,128)(2,1)S(1)} %add_convert_fusion.3), channel_id=1, source_target_pairs={{4,0},{8,12},{5,1},{9,13},{6,2},{10,14},{7,3},{11,15},{20,16},{24,... | collective-permute-start | bytes 2457608 | tf_op jit(solution)/shard_map/ppermute | solution.py:783
  575.9 97.7 %collective-permute-start.111 = (bf16[320,1280]{1,0:T(8,128)(2,1)S(1)}, bf16[320,1280]{1,0:T(8,128)(2,1)S(1)}, u32[]{:S(2)}, u32[]{:S(2)}) collective-permute-start(bf16[320,1280]{1,0:T(8,128)(2,1)S(1)} %add_convert_fusion.5), channel_id=1, source_target_pairs={{4,0},{8,12},{5,1},{9,13},{6,2},{10,14},{7,3},{11,15},{20,16},{24,... | collective-permute-start | bytes 2457608 | tf_op jit(solution)/shard_map/ppermute | solution.py:783
  577.2 91.2 %collective-permute-start.108 = (bf16[640,320]{0,1:T(8,128)(2,1)S(1)}, bf16[640,320]{0,1:T(8,128)(2,1)S(1)}, u32[]{:S(2)}, u32[]{:S(2)}) collective-permute-start(bf16[640,320]{0,1:T(8,128)(2,1)S(1)} %add_convert_fusion.10), channel_id=1, source_target_pairs={{4,0},{8,12},{5,1},{9,13},{6,2},{10,14},{7,3},{11,15},{20,16},{24,... | collective-permute-start | bytes 1228808 | tf_op jit(solution)/shard_map/ppermute | solution.py:783
  (183 other events, 1760.5 us)

commit v2 on v1

--- a/solution.py
+++ b/solution.py
@@ -721,7 +721,6 @@
         )
         s.plan = jnp.concatenate([jnp.sum(live)[None], listed]).astype(jnp.int32)
     every = lambda name: [getattr(s, name) for s in state]
-    last = state[-1]
 
     def tied(values, *others):
         return list(lax.optimization_barrier((tuple(values),) + others)[0])
@@ -782,7 +781,7 @@
     def hop(stage, values):
         return [lax.ppermute(v, "ctx", hops[stage]) for v in values]
 
-    def plus(values, others):
+    def plain_plus(values, others):
         return [(a.astype(F32) + b.astype(F32)).astype(BF) for a, b in zip(values, others)]
 
     def finish(whole, third):
@@ -805,8 +804,8 @@
         previous = (low_middle,)
         s.low_parts = spread_rows(low_middle)
         if m == 0:
-            outer = weight_grad(every("low"), every("active"))
-            inner = weight_grad(every("normed_two"), every("inner"))
+            outer = weight_grad(every("low"), tied(every("active"), low_middle))
+    inner = weight_grad(every("normed_two"), tied(every("inner"), *previous))
     previous = ()
     for m in range(micros):
         s = state[m]
@@ -835,44 +834,57 @@
         previous = (s.gq,)
         s.parts_one = found[5:]
     names = "kvq"
-    three = {
-        n: weight_grad(every("normed"), every(g)) for n, g in zip(names, ("gk", "gv", "gq"))
-    }
+    three = {}
+    for n, g in zip(names, ("gk", "gv", "gq")):
+        three[n] = weight_grad(every("normed"), every(g))
+    homes = [three[n][0] for n in names]
+    outer = plain_plus(outer, tied(outer_first, *homes))
+    outer_second = hop(1, outer)
+    inner = plain_plus(inner, tied(inner_first, *outer))
+    inner_second = hop(1, inner)
+    output = plain_plus(output, tied(output_first, *inner))
+    output_second = hop(1, output)
+    token = output
+    three_first = {}
+    for n in names:
+        three[n] = [joined(tied(three[n], *token))]
+        three_first[n] = hop(0, three[n])
+        token = three[n]
+        if n == "k":
+            outer = plain_plus(outer, tied(outer_second, *token))
+            outer_third = hop(2, outer)
+            token = outer
+    early = token
+    three_second = {}
+    for n in names:
+        three[n] = plain_plus(three[n], tied(three_first[n], *token))
+        three_second[n] = hop(1, three[n])
+        token = three[n]
     for m in range(micros):
         s = state[m]
         out, s.gain_one, s.bias_one = first_back(
-            *reduce_rows(s.parts_one), s.own, s.grad_middle, gain_one
+            *tied(reduce_rows(s.parts_one), *token), s.own, s.grad_middle, gain_one
         )
         s.frames_grad = spread_rows(out)
-    outer = plus(outer, outer_first)
-    outer_second = hop(1, outer)
-    three = {n: [joined(tied(three[n], *outer))] for n in names}
-    three_first = {n: hop(0, three[n]) for n in names}
-    gate = [three[n][0] for n in names]
-    inner = plus(inner, tied(inner_first, *gate))
-    inner_second = hop(1, inner)
-    output = plus(output, tied(output_first, *gate))
-    output_second = hop(1, output)
-    outer = plus(outer, tied(outer_second, *inner))
-    outer_third = hop(2, outer)
-    three = {n: plus(three[n], tied(three_first[n], *outer)) for n in names}
-    three_second = {n: hop(1, three[n]) for n in names}
-    gate = [three[n][0] for n in names]
-    inner = plus(inner, tied(inner_second, *gate))
+    inner = plain_plus(inner, tied(inner_second, *token))
     inner_third = hop(2, inner)
-    output = plus(output, tied(output_second, *gate))
+    output = plain_plus(output, tied(output_second, *inner))
     output_third = hop(2, output)
-    three = {n: plus(three[n], tied(three_second[n], *inner)) for n in names}
-    three_third = {n: hop(2, three[n]) for n in names}
-    for m in range(micros):
-        s = state[m]
-        keep, near, far = reduce_rows(tied(s.forward, last.slabs_back[0]))
+    token = output
+    three_third = {}
+    for n in names:
+        three[n] = plain_plus(three[n], tied(three_second[n], *token))
+        three_third[n] = hop(2, three[n])
+        token = three[n]
+    for m in range(micros):
+        s = state[m]
+        keep, near, far = reduce_rows(tied(s.forward, *early))
         final = (
             s.middle + (keep + near.astype(F32) + far.astype(F32)) + outer_shift
         ).astype(BF)
         s.result = spread_rows(final)
-    result = gather_rows(ids, sum((s.result for s in state), ()))
-    frames_grad = gather_rows(ids, sum((s.frames_grad for s in state), ()))
+    result = gather_rows(ids, tied(sum((s.result for s in state), ()), *inner))
+    frames_grad = gather_rows(ids, tied(sum((s.frames_grad for s in state), ()), *output))
     grads["f"] = finish(outer, outer_third)
     grads["i"] = finish(inner, inner_third)
     grads["o"] = finish(output, output_third)
@@ -885,8 +897,9 @@
 
     def over_frames(value):
         value = value + mate(value) if paired else lax.psum(value, "shard")
-        value = value + blocks(value, 1)
-        return value + blocks(value, 2)
+        other = blocks(value, 1)
+        value = value + other
+        return value + blocks(tie(value, *token), 2)
 
     def both(name):
         return sum(every(name))

time: 700 us -> 706 us (level)
  starting transfers between devices: 136 us -> 162 us
  waiting for transfers between devices: 283 us -> 264 us
    ppermute x26, starting transfers between devices: 53.6 us -> 70.3 us  [blocks(): return lax.ppermute(value, 'ctx', [(i, i ^ slot) for i in range(4)])]
    ppermute x17, waiting for transfers between devices: 35.9 us -> 23.8 us  [across(): return lax.ppermute(value, 'tp', [(i, i ^ 2) for i in range(4)])]
    ppermute x26, waiting for transfers between devices: 38.4 us -> 30.3 us  [blocks(): return lax.ppermute(value, 'ctx', [(i, i ^ slot) for i in range(4)])]
    ppermute x24, starting transfers between devices: 39.4 us -> 47.5 us  [hop(): return [lax.ppermute(v, 'ctx', hops[stage]) for v in values]]
    unnamed x240 -> x216, local copies, waits for them, and re-layouts: 15.1 us -> 16.3 us
  transfers between devices with their start and end apart: 113 -> 113, of which waited for: 28 -> 33; matrix products, arithmetic and copies ran while one was open for 17% -> 16% of each run, Pallas kernels for 19% -> 18%
where the time goes in v2:
time: 706 us; the launch traced here: 697 us
  waiting for transfers between devices  264 us (37%)
  starting transfers between devices  162 us (23%)
  Pallas kernels  141 us (20%)
  other arithmetic  53.8 us (8%)
  matrix products  39.1 us (6%)
  local copies, waits for them, and re-layouts  34.1 us (5%)
    ppermute x24, waiting for transfers between devices, hop(): return [lax.ppermute(v, 'ctx', hops[stage]) for v in values]  142 us
    ppermute x26, starting transfers between devices, blocks(): return lax.ppermute(value, 'ctx', [(i, i ^ slot) for i in range(4)])  70.3 us
    ppermute x13, waiting for transfers between devices, mate(): return lax.ppermute(value, 'shard', [(0, 1), (1, 0)])  66.9 us
    ppermute x24, starting transfers between devices, hop(): return [lax.ppermute(v, 'ctx', hops[stage]) for v in values]  47.5 us
    dot_general x24, matrix products, dot_tn(): return lax.dot_general(left, right, TN, preferred_element_type=F32)  39.1 us
    pallas_call x2, Pallas kernels, feed(): pl.pallas_call(feed_kernel, grid=(hidden // block,), out_shape=(sds((rows...  32.2 us
    ppermute x26, waiting for transfers between devices, blocks(): return lax.ppermute(value, 'ctx', [(i, i ^ slot) for i in range(4)])  30.3 us
    ppermute x17, waiting for transfers between devices, across(): return lax.ppermute(value, 'tp', [(i, i ^ 2) for i in range(4)])  23.8 us
  transfers between devices with their start and end apart: 113, of which 33 were waited for; matrix products, arithmetic and copies ran while one was open for 16% of the time, Pallas kernels for 18%

profile of v2, /device:TPU:0, one launch (start us, length us, event | category | flops | bytes accessed | tf_op | source)
XLA Modules:
  0.0 696.8 jit_solution(14216149854227615786)
XLA Ops:
  13.9 5.4 shard_map.306
  19.3 5.5 shard_map.305
  37.5 5.7 shard_map.307
  48.4 5.7 shard_map.308
  61.1 14.8 %collective-permute-done.4.x2 = bf16[240,512]{1,0:T(8,128)(2,1)S(1)} collective-permute-done((bf16[240,512]{1,0:T(8,128)(2,1)}, bf16[240,512]{1,0:T(8,128)(2,1)S(1)}, u32[]{:S(2)}, u32[]{:S(2)}) %collective-permute-start.4) | collective-permute-done | bytes 245792 | tf_op jit(solution)/shard_map/ppermute | solution.py:623
  81.5 3.6 collective-permute-start.6
  93.3 10.0 %shard_map.310 = (bf16[80,512]{1,0:T(8,128)(2,1)}, bf16[80,512]{1,0:T(8,128)(2,1)}, bf16[80,512]{1,0:T(8,128)(2,1)}, bf16[80,512]{1,0:T(8,128)(2,1)}, f32[4,80,512]{2,1,0:T(8,128)}, /*index=5*/f32[4,1,512]{2,1,0:T(1,128)}) custom-call(s32[5]{0:T(128)} %pad_add_fusion.4.plan, bf16[240,512]{1,0:T(8,128)(2,1)} %get-tuple-element.275.x0, ...), custom_call_target="tpu_custom_call" | custom-call | tf_op jit(solution)/shard_map/pallas_call | solution.py:172
  104.8 3.6 shard_map.311
  108.4 5.4 collective-permute-start.30
  118.4 4.4 collective-permute-done.31.m2
  123.5 3.6 shard_map.316
  145.5 7.6 %collective-permute-done.16.n1 = bf16[128,1280]{1,0:T(8,128)(2,1)} collective-permute-done((bf16[128,1280]{1,0:T(8,128)(2,1)}, bf16[128,1280]{1,0:T(8,128)(2,1)}, u32[]{:S(2)}, u32[]{:S(2)}) %collective-permute-start.16) | collective-permute-done | bytes 327712 | tf_op jit(solution)/shard_map/ppermute | solution.py:620
  155.0 3.3 collective-permute-done.35.second
  163.1 26.1 %collective-permute-done.20.ob = bf16[640,1280]{1,0:T(8,128)(2,1)} collective-permute-done((bf16[640,1280]{1,0:T(8,128)(2,1)}, bf16[640,1280]{1,0:T(8,128)(2,1)}, u32[]{:S(2)}, u32[]{:S(2)}) %collective-permute-start.20) | collective-permute-done | bytes 1638432 | tf_op jit(solution)/shard_map/ppermute | solution.py:626
  189.2 15.9 %shard_map.313 = (bf16[512,1280]{1,0:T(8,128)(2,1)}, bf16[512,1280]{1,0:T(8,128)(2,1)}, bf16[512,1280]{1,0:T(8,128)(2,1)}, f32[1,1280]{1,0:T(1,128)}, f32[128,12...) custom-call(bf16[128,1280]{1,0:T(8,128)(2,1)} %get-tuple-element.291, ...), custom_call_target="tpu_custom_call" | custom-call | tf_op jit(solution)/shard_map/pallas_call | solution.py:408
  211.2 16.3 %shard_map.318 = (bf16[512,1280]{1,0:T(8,128)(2,1)}, bf16[512,1280]{1,0:T(8,128)(2,1)}, bf16[512,1280]{1,0:T(8,128)(2,1)}, f32[1,1280]{1,0:T(1,128)}, f32[128,12...) custom-call(bf16[128,1280]{1,0:T(8,128)(2,1)} %get-tuple-element.331, ...), custom_call_target="tpu_custom_call" | custom-call | tf_op jit(solution)/shard_map/pallas_call | solution.py:408
  240.4 9.2 %collective-permute-done.41.second = bf16[128,1280]{1,0:T(8,128)(2,1)S(1)} collective-permute-done((bf16[128,1280]{1,0:T(8,128)(2,1)S(1)}, bf16[128,1280]{1,0:T(8,128)(2,1)S(1)}, u32[]{:S(2)}, u32[]{:S(2)}) %collective-permute-start.41) | collective-permute-done | bytes 327712 | tf_op jit(solution)/shard_map/ppermute | solution.py:620
  265.6 3.3 shard_map.315
  273.3 4.7 fusion.1
  278.1 3.5 shard_map.320
  286.1 3.7 shard_map.321
  298.7 15.9 %shard_map.323 = (bf16[240,512]{1,0:T(8,128)(2,1)}, bf16[240,512]{1,0:T(8,128)(2,1)}, bf16[240,512]{1,0:T(8,128)(2,1)}, bf16[240,512]{1,0:T(8,128)(2,1)}) custom-call(s32[5]{0:T(128)} %pad_add_fusion.4.plan, bf16[240,512]{1,0:T(8,128)(2,1)} %get-tuple-element.275.x0, bf16[240,512]{1,0:T(8,128)(2,1)} %copy-done.38, bf16[240,512]{1,0:T(8,128)(2,1)} %copy-done.36, ...), custom_call_target="tpu_custom_call" | custom-call | tf_op jit(solution)/shard_map/pallas_call | solution.py:264
  323.7 5.9 shard_map.322
  331.6 4.3 collective-permute-done.52.s2
  336.4 6.0 shard_map.324
  362.6 9.3 %collective-permute-start.57 = (bf16[320,1280]{1,0:T(8,128)(2,1)S(1)}, bf16[320,1280]{1,0:T(8,128)(2,1)S(1)}, u32[]{:S(2)}, u32[]{:S(2)}) collective-permute-start(bf16[320,1280]{1,0:T(8,128)(2,1)S(1)} %get-tuple-element.525), channel_id=1, source_target_pairs={{0,4},{12,8},{1,5},{13,9},{2,6},{14,10},{3,7},{15,11},{16,20},{28,... | collective-permute-start | bytes 2457608 | tf_op jit(solution)/shard_map/ppermute | solution.py:782
  373.4 22.3 %collective-permute-done.63 = bf16[640,1280]{1,0:T(8,128)(2,1)} collective-permute-done((bf16[640,1280]{1,0:T(8,128)(2,1)}, bf16[640,1280]{1,0:T(8,128)(2,1)}, u32[]{:S(2)}, u32[]{:S(2)}) %collective-permute-start.63) | collective-permute-done | bytes 1638432 | tf_op jit(solution)/shard_map/ppermute | solution.py:626
  404.5 3.5 collective-permute-done.58
  408.0 4.4 collective-permute-start.64
  412.8 12.8 %collective-permute-done.65 = bf16[320,1280]{1,0:T(8,128)(2,1)S(1)} collective-permute-done((bf16[320,1280]{1,0:T(8,128)(2,1)S(1)}, bf16[320,1280]{1,0:T(8,128)(2,1)S(1)}, u32[]{:S(2)}, u32[]{:S(2)}) %collective-permute-start.65) | collective-permute-done | bytes 819232 | tf_op jit(solution)/shard_map/ppermute | solution.py:782
  426.3 16.8 %collective-permute-done.66 = bf16[320,1280]{1,0:T(8,128)(2,1)S(1)} collective-permute-done((bf16[320,1280]{1,0:T(8,128)(2,1)S(1)}, bf16[320,1280]{1,0:T(8,128)(2,1)S(1)}, u32[]{:S(2)}, u32[]{:S(2)}) %collective-permute-start.66) | collective-permute-done | bytes 819232 | tf_op jit(solution)/shard_map/ppermute | solution.py:782
  444.4 6.6 collective-permute-done.64
  451.0 3.2 collective-permute-start.55
  456.2 8.3 %collective-permute-done.55 = bf16[640,320]{0,1:T(8,128)(2,1)S(1)} collective-permute-done((bf16[640,320]{0,1:T(8,128)(2,1)S(1)}, bf16[640,320]{0,1:T(8,128)(2,1)S(1)}, u32[]{:S(2)}, u32[]{:S(2)}) %collective-permute-start.55) | collective-permute-done | bytes 409632 | tf_op jit(solution)/shard_map/ppermute | solution.py:626
  466.1 6.2 collective-permute-done.54
  472.3 4.4 collective-permute-start.83
  477.0 7.6 %collective-permute-done.83 = bf16[640,320]{0,1:T(8,128)(2,1)S(1)} collective-permute-done((bf16[640,320]{0,1:T(8,128)(2,1)S(1)}, bf16[640,320]{0,1:T(8,128)(2,1)S(1)}, u32[]{:S(2)}, u32[]{:S(2)}) %collective-permute-start.83) | collective-permute-done | bytes 409632 | tf_op jit(solution)/shard_map/ppermute | solution.py:782
  484.6 4.4 collective-permute-start.82
  492.0 6.8 collective-permute-done.82
  501.1 3.7 collective-permute-done.81
  531.4 30.5 %collective-permute-start.100 = (f32[8,1280]{1,0:T(8,128)S(1)}, f32[8,1280]{1,0:T(8,128)S(1)}, u32[]{:S(2)}, u32[]{:S(2)}) collective-permute-start(f32[8,1280]{1,0:T(8,128)S(1)} %add.349), channel_id=1, source_target_pairs={{0,4},{4,0},{8,12},{12,8},{1,5},{5,1},{9,13},{13,9},{2,6},{6,2},{1... | collective-permute-start | bytes 122888 | tf_op jit(solution)/shard_map/ppermute | solution.py:623
  572.4 14.5 %collective-permute-done.111 = bf16[320,1280]{1,0:T(8,128)(2,1)S(1)} collective-permute-done((bf16[320,1280]{1,0:T(8,128)(2,1)S(1)}, bf16[320,1280]{1,0:T(8,128)(2,1)S(1)}, u32[]{:S(2)}, u32[]{:S(2)}) %collective-permute-start.111) | collective-permute-done | bytes 819232 | tf_op jit(solution)/shard_map/ppermute | solution.py:782
  587.7 16.8 %collective-permute-done.112 = bf16[320,1280]{1,0:T(8,128)(2,1)S(1)} collective-permute-done((bf16[320,1280]{1,0:T(8,128)(2,1)S(1)}, bf16[320,1280]{1,0:T(8,128)(2,1)S(1)}, u32[]{:S(2)}, u32[]{:S(2)}) %collective-permute-start.112) | collective-permute-done | bytes 819232 | tf_op jit(solution)/shard_map/ppermute | solution.py:782
  609.5 20.4 %collective-permute-done.108 = bf16[640,320]{0,1:T(8,128)(2,1)S(1)} collective-permute-done((bf16[640,320]{0,1:T(8,128)(2,1)S(1)}, bf16[640,320]{0,1:T(8,128)(2,1)S(1)}, u32[]{:S(2)}, u32[]{:S(2)}) %collective-permute-start.108) | collective-permute-done | bytes 409632 | tf_op jit(solution)/shard_map/ppermute | solution.py:782
  644.5 5.7 shard_map.328
  652.7 18.8 %collective-permute-done.107 = bf16[640,320]{0,1:T(8,128)(2,1)S(1)} collective-permute-done((bf16[640,320]{0,1:T(8,128)(2,1)S(1)}, bf16[640,320]{0,1:T(8,128)(2,1)S(1)}, u32[]{:S(2)}, u32[]{:S(2)}) %collective-permute-start.107) | collective-permute-done | bytes 409632 | tf_op jit(solution)/shard_map/ppermute | solution.py:782
  674.6 11.7 %collective-permute-done.105 = bf16[640,320]{0,1:T(8,128)(2,1)S(1)} collective-permute-done((bf16[640,320]{0,1:T(8,128)(2,1)S(1)}, bf16[640,320]{0,1:T(8,128)(2,1)S(1)}, u32[]{:S(2)}, u32[]{:S(2)}) %collective-permute-start.105) | collective-permute-done | bytes 409632 | tf_op jit(solution)/shard_map/ppermute | solution.py:782
  690.7 5.7 shard_map.325
  (573 shorter events, 256.1 us)
Async XLA Ops:
  2.0 35.5 %collective-permute-start.2 = (bf16[640,320]{1,0:T(8,128)(2,1)S(1)}, bf16[640,320]{1,0:T(8,128)(2,1)}, u32[]{:S(2)}, u32[]{:S(2)}) collective-permute-start(bf16[640,320]{1,0:T(8,128)(2,1)S(1)} %copy.60.va), channel_id=1, source_target_pairs={{0,16},{16,0},{1,17},{17,1},{2,18},{18,2},{3,19},{19,3},{4,20},{20... | collective-permute-start | bytes 1228808 | tf_op jit(solution)/shard_map/ppermute | solution.py:626
  7.1 30.4 %collective-permute-start = (bf16[640,320]{1,0:T(8,128)(2,1)}, bf16[640,320]{1,0:T(8,128)(2,1)}, u32[]{:S(2)}, u32[]{:S(2)}) collective-permute-start(bf16[640,320]{1,0:T(8,128)(2,1)} %copy.58.qa), channel_id=1, source_target_pairs={{0,16},{16,0},{1,17},{17,1},{2,18},{18,2},{3,19},{19,3},{4,20},{20... | collective-permute-start | bytes 1228808 | tf_op jit(solution)/shard_map/ppermute | solution.py:626
  8.2 29.3 %collective-permute-start.1 = (bf16[640,320]{1,0:T(8,128)(2,1)}, bf16[640,320]{1,0:T(8,128)(2,1)}, u32[]{:S(2)}, u32[]{:S(2)}) collective-permute-start(bf16[640,320]{1,0:T(8,128)(2,1)} %copy.59.ka), channel_id=1, source_target_pairs={{0,16},{16,0},{1,17},{17,1},{2,18},{18,2},{3,19},{19,3},{4,20},{20... | collective-permute-start | bytes 1228808 | tf_op jit(solution)/shard_map/ppermute | solution.py:626
  44.9 31.0 %collective-permute-start.4 = (bf16[240,512]{1,0:T(8,128)(2,1)}, bf16[240,512]{1,0:T(8,128)(2,1)S(1)}, u32[]{:S(2)}, u32[]{:S(2)}) collective-permute-start(bf16[240,512]{1,0:T(8,128)(2,1)} %get-tuple-element.259), channel_id=1, source_target_pairs={{0,8},{4,12},{8,0},{12,4},{1,9},{5,13},{9,1},{13,5},{2,10},{6,14},... | collective-permute-start | bytes 737288 | tf_op jit(solution)/shard_map/ppermute | solution.py:623
  48.3 29.9 %collective-permute-start.5 = (bf16[240,512]{1,0:T(8,128)(2,1)}, bf16[240,512]{1,0:T(8,128)(2,1)S(1)}, u32[]{:S(2)}, u32[]{:S(2)}) collective-permute-start(bf16[240,512]{1,0:T(8,128)(2,1)} %get-tuple-element.260), channel_id=1, source_target_pairs={{0,12},{4,8},{8,4},{12,0},{1,13},{5,9},{9,5},{13,1},{2,14},{6,10},... | collective-permute-start | bytes 737288 | tf_op jit(solution)/shard_map/ppermute | solution.py:623
  54.1 34.1 %collective-permute-start.10 = (bf16[240,512]{1,0:T(8,128)(2,1)}, bf16[240,512]{1,0:T(8,128)(2,1)S(1)}, u32[]{:S(2)}, u32[]{:S(2)}) collective-permute-start(bf16[240,512]{1,0:T(8,128)(2,1)} %get-tuple-element.273), channel_id=1, source_target_pairs={{0,8},{4,12},{8,0},{12,4},{1,9},{5,13},{9,1},{13,5},{2,10},{6,14},... | collective-permute-start | bytes 737288 | tf_op jit(solution)/shard_map/ppermute | solution.py:623
  56.0 32.2 %collective-permute-start.11 = (bf16[240,512]{1,0:T(8,128)(2,1)}, bf16[240,512]{1,0:T(8,128)(2,1)S(1)}, u32[]{:S(2)}, u32[]{:S(2)}) collective-permute-start(bf16[240,512]{1,0:T(8,128)(2,1)} %get-tuple-element.274), channel_id=1, source_target_pairs={{0,12},{4,8},{8,4},{12,0},{1,13},{5,9},{9,5},{13,1},{2,14},{6,10},... | collective-permute-start | bytes 737288 | tf_op jit(solution)/shard_map/ppermute | solution.py:623
  59.0 44.3 %collective-permute-start.12 = (bf16[640,320]{1,0:T(8,128)(2,1)}, bf16[640,320]{1,0:T(8,128)(2,1)S(1)}, u32[]{:S(2)}, u32[]{:S(2)}) collective-permute-start(bf16[640,320]{1,0:T(8,128)(2,1)} %copy.64), channel_id=1, source_target_pairs={{0,16},{16,0},{1,17},{17,1},{2,18},{18,2},{3,19},{19,3},{4,20},{20... | collective-permute-start | bytes 1228808 | tf_op jit(solution)/shard_map/ppermute | solution.py:626
  116.3 46.8 %collective-permute-start.19 = (bf16[640,1280]{1,0:T(8,128)(2,1)S(1)}, bf16[640,1280]{1,0:T(8,128)(2,1)}, u32[]{:S(2)}, u32[]{:S(2)}) collective-permute-start(bf16[640,1280]{1,0:T(8,128)(2,1)S(1)} %copy-done.9), channel_id=1, source_target_pairs={{0,16},{16,0},{1,17},{17,1},{2,18},{18,2},{3,19},{19,3},{4,20},{20... | collective-permute-start | bytes 4915208 | tf_op jit(solution)/shard_map/ppermute | solution.py:626
  116.9 72.3 %collective-permute-start.20 = (bf16[640,1280]{1,0:T(8,128)(2,1)}, bf16[640,1280]{1,0:T(8,128)(2,1)}, u32[]{:S(2)}, u32[]{:S(2)}) collective-permute-start(bf16[640,1280]{1,0:T(8,128)(2,1)} %oa.3), channel_id=1, source_target_pairs={{0,16},{16,0},{1,17},{17,1},{2,18},{18,2},{3,19},{19,3},{4,20},{20... | collective-permute-start | bytes 4915208 | tf_op jit(solution)/shard_map/ppermute | solution.py:626
  161.5 44.4 %collective-permute-start.36 = (bf16[128,1280]{1,0:T(8,128)(2,1)}, bf16[128,1280]{1,0:T(8,128)(2,1)}, u32[]{:S(2)}, u32[]{:S(2)}) collective-permute-start(bf16[128,1280]{1,0:T(8,128)(2,1)} %get-tuple-element.331.n0), channel_id=1, source_target_pairs={{0,2},{1,3},{2,0},{3,1},{4,6},{5,7},{6,4},{7,5},{8,10},{9,11},{10,... | collective-permute-start | bytes 983048 | tf_op jit(solution)/shard_map/ppermute | solution.py:620
  206.0 23.5 %collective-permute-start.21 = (bf16[128,1280]{1,0:T(8,128)(2,1)}, bf16[128,1280]{1,0:T(8,128)(2,1)}, u32[]{:S(2)}, u32[]{:S(2)}) collective-permute-start(bf16[128,1280]{1,0:T(8,128)(2,1)} %get-tuple-element.303), channel_id=1, source_target_pairs={{0,1},{1,0},{2,3},{3,2},{4,5},{5,4},{6,7},{7,6},{8,9},{9,8},{10,11... | collective-permute-start | bytes 983048 | tf_op jit(solution)/shard_map/ppermute | solution.py:617
  232.6 29.7 %collective-permute-start.24 = (bf16[128,1280]{1,0:T(8,128)(2,1)}, bf16[128,1280]{1,0:T(8,128)(2,1)}, u32[]{:S(2)}, u32[]{:S(2)}) collective-permute-start(bf16[128,1280]{1,0:T(8,128)(2,1)} %get-tuple-element.310.l0), channel_id=1, source_target_pairs={{0,2},{1,3},{2,0},{3,1},{4,6},{5,7},{6,4},{7,5},{8,10},{9,11},{10,... | collective-permute-start | bytes 983048 | tf_op jit(solution)/shard_map/ppermute | solution.py:620
  233.2 32.4 %collective-permute-start.25 = (bf16[128,1280]{1,0:T(8,128)(2,1)}, bf16[128,1280]{1,0:T(8,128)(2,1)}, u32[]{:S(2)}, u32[]{:S(2)}) collective-permute-start(bf16[128,1280]{1,0:T(8,128)(2,1)} %get-tuple-element.310.l0), channel_id=1, source_target_pairs={{0,1},{1,0},{2,3},{3,2},{4,5},{5,4},{6,7},{7,6},{8,9},{9,8},{10,11... | collective-permute-start | bytes 983048 | tf_op jit(solution)/shard_map/ppermute | solution.py:617
  254.0 24.0 %collective-permute-start.43 = (bf16[128,1280]{1,0:T(8,128)(2,1)}, bf16[128,1280]{1,0:T(8,128)(2,1)}, u32[]{:S(2)}, u32[]{:S(2)}) collective-permute-start(bf16[128,1280]{1,0:T(8,128)(2,1)} %get-tuple-element.345.l0), channel_id=1, source_target_pairs={{0,1},{1,0},{2,3},{3,2},{4,5},{5,4},{6,7},{7,6},{8,9},{9,8},{10,11... | collective-permute-start | bytes 983048 | tf_op jit(solution)/shard_map/ppermute | solution.py:617
  289.7 26.9 %collective-permute-start.45 = (bf16[240,512]{1,0:T(8,128)(2,1)}, bf16[240,512]{1,0:T(8,128)(2,1)S(1)}, u32[]{:S(2)}, u32[]{:S(2)}) collective-permute-start(bf16[240,512]{1,0:T(8,128)(2,1)} %get-tuple-element.357), channel_id=1, source_target_pairs={{0,4},{4,0},{8,12},{12,8},{1,5},{5,1},{9,13},{13,9},{2,6},{6,2},{1... | collective-permute-start | bytes 737288 | tf_op jit(solution)/shard_map/ppermute | solution.py:623
  294.4 27.3 %collective-permute-start.46 = (bf16[240,512]{1,0:T(8,128)(2,1)}, bf16[240,512]{1,0:T(8,128)(2,1)}, u32[]{:S(2)}, u32[]{:S(2)}) collective-permute-start(bf16[240,512]{1,0:T(8,128)(2,1)} %get-tuple-element.358), channel_id=1, source_target_pairs={{0,8},{4,12},{8,0},{12,4},{1,9},{5,13},{9,1},{13,5},{2,10},{6,14},... | collective-permute-start | bytes 737288 | tf_op jit(solution)/shard_map/ppermute | solution.py:623
  296.3 27.3 %collective-permute-start.47 = (bf16[240,512]{1,0:T(8,128)(2,1)}, bf16[240,512]{1,0:T(8,128)(2,1)}, u32[]{:S(2)}, u32[]{:S(2)}) collective-permute-start(bf16[240,512]{1,0:T(8,128)(2,1)} %get-tuple-element.359), channel_id=1, source_target_pairs={{0,12},{4,8},{8,4},{12,0},{1,13},{5,9},{9,5},{13,1},{2,14},{6,10},... | collective-permute-start | bytes 737288 | tf_op jit(solution)/shard_map/ppermute | solution.py:623
  321.7 39.0 %collective-permute-start.56 = (bf16[640,1280]{1,0:T(8,128)(2,1)}, bf16[640,1280]{1,0:T(8,128)(2,1)}, u32[]{:S(2)}, u32[]{:S(2)}) collective-permute-start(bf16[640,1280]{1,0:T(8,128)(2,1)} %fusion), channel_id=1, source_target_pairs={{0,16},{16,0},{1,17},{17,1},{2,18},{18,2},{3,19},{19,3},{4,20},{20... | collective-permute-start | bytes 4915208 | tf_op jit(solution)/shard_map/ppermute | solution.py:626
  323.6 72.2 %collective-permute-start.63 = (bf16[640,1280]{1,0:T(8,128)(2,1)}, bf16[640,1280]{1,0:T(8,128)(2,1)}, u32[]{:S(2)}, u32[]{:S(2)}) collective-permute-start(bf16[640,1280]{1,0:T(8,128)(2,1)} %fusion.1), channel_id=1, source_target_pairs={{0,16},{16,0},{1,17},{17,1},{2,18},{18,2},{3,19},{19,3},{4,20},{20... | collective-permute-start | bytes 4915208 | tf_op jit(solution)/shard_map/ppermute | solution.py:626
  329.7 71.9 %collective-permute-start.62 = (bf16[640,320]{0,1:T(8,128)(2,1)}, bf16[640,320]{0,1:T(8,128)(2,1)}, u32[]{:S(2)}, u32[]{:S(2)}) collective-permute-start(bf16[640,320]{0,1:T(8,128)(2,1)} %fusion.5), channel_id=1, source_target_pairs={{0,16},{16,0},{1,17},{17,1},{2,18},{18,2},{3,19},{19,3},{4,20},{20... | collective-permute-start | bytes 1228808 | tf_op jit(solution)/shard_map/ppermute | solution.py:626
  335.9 174.3 %collective-permute-start.84 = (bf16[128,1280]{1,0:T(8,128)(2,1)}, bf16[128,1280]{1,0:T(8,128)(2,1)}, u32[]{:S(2)}, u32[]{:S(2)}) collective-permute-start(bf16[128,1280]{1,0:T(8,128)(2,1)} %get-tuple-element.445), channel_id=1, source_target_pairs={{0,1},{1,0},{2,3},{3,2},{4,5},{5,4},{6,7},{7,6},{8,9},{9,8},{10,11... | collective-permute-start | bytes 983048 | tf_op jit(solution)/shard_map/ppermute | solution.py:617
  362.6 41.5 %collective-permute-start.57 = (bf16[320,1280]{1,0:T(8,128)(2,1)S(1)}, bf16[320,1280]{1,0:T(8,128)(2,1)S(1)}, u32[]{:S(2)}, u32[]{:S(2)}) collective-permute-start(bf16[320,1280]{1,0:T(8,128)(2,1)S(1)} %get-tuple-element.525), channel_id=1, source_target_pairs={{0,4},{12,8},{1,5},{13,9},{2,6},{14,10},{3,7},{15,11},{16,20},{28,... | collective-permute-start | bytes 2457608 | tf_op jit(solution)/shard_map/ppermute | solution.py:782
  371.9 36.1 %collective-permute-start.58 = (bf16[320,1280]{1,0:T(8,128)(2,1)S(1)}, bf16[320,1280]{1,0:T(8,128)(2,1)S(1)}, u32[]{:S(2)}, u32[]{:S(2)}) collective-permute-start(bf16[320,1280]{1,0:T(8,128)(2,1)S(1)} %get-tuple-element.524), channel_id=1, source_target_pairs={{0,4},{12,8},{1,5},{13,9},{2,6},{14,10},{3,7},{15,11},{16,20},{28,... | collective-permute-start | bytes 2457608 | tf_op jit(solution)/shard_map/ppermute | solution.py:782
  397.7 27.9 %collective-permute-start.65 = (bf16[320,1280]{1,0:T(8,128)(2,1)S(1)}, bf16[320,1280]{1,0:T(8,128)(2,1)S(1)}, u32[]{:S(2)}, u32[]{:S(2)}) collective-permute-start(bf16[320,1280]{1,0:T(8,128)(2,1)S(1)} %get-tuple-element.521), channel_id=1, source_target_pairs={{0,4},{12,8},{1,5},{13,9},{2,6},{14,10},{3,7},{15,11},{16,20},{28,... | collective-permute-start | bytes 2457608 | tf_op jit(solution)/shard_map/ppermute | solution.py:782
  401.6 41.5 %collective-permute-start.66 = (bf16[320,1280]{1,0:T(8,128)(2,1)S(1)}, bf16[320,1280]{1,0:T(8,128)(2,1)S(1)}, u32[]{:S(2)}, u32[]{:S(2)}) collective-permute-start(bf16[320,1280]{1,0:T(8,128)(2,1)S(1)} %get-tuple-element.520), channel_id=1, source_target_pairs={{0,4},{12,8},{1,5},{13,9},{2,6},{14,10},{3,7},{15,11},{16,20},{28,... | collective-permute-start | bytes 2457608 | tf_op jit(solution)/shard_map/ppermute | solution.py:782
  404.1 51.0 %collective-permute-start.61 = (bf16[640,320]{0,1:T(8,128)(2,1)S(1)}, bf16[640,320]{0,1:T(8,128)(2,1)S(1)}, u32[]{:S(2)}, u32[]{:S(2)}) collective-permute-start(bf16[640,320]{0,1:T(8,128)(2,1)S(1)} %copy-done.54), channel_id=1, source_target_pairs={{0,16},{16,0},{1,17},{17,1},{2,18},{18,2},{3,19},{19,3},{4,20},{20... | collective-permute-start | bytes 1228808 | tf_op jit(solution)/shard_map/ppermute | solution.py:626
  408.0 43.0 %collective-permute-start.64 = (bf16[640,320]{0,1:T(8,128)(2,1)S(1)}, bf16[640,320]{0,1:T(8,128)(2,1)S(1)}, u32[]{:S(2)}, u32[]{:S(2)}) collective-permute-start(bf16[640,320]{0,1:T(8,128)(2,1)S(1)} %add_convert_fusion.21), channel_id=1, source_target_pairs={{0,4},{12,8},{1,5},{13,9},{2,6},{14,10},{3,7},{15,11},{16,20},{28,... | collective-permute-start | bytes 1228808 | tf_op jit(solution)/shard_map/ppermute | solution.py:782
  425.6 29.6 %collective-permute-start.59 = (bf16[320,1280]{1,0:T(8,128)(2,1)S(1)}, bf16[320,1280]{1,0:T(8,128)(2,1)S(1)}, u32[]{:S(2)}, u32[]{:S(2)}) collective-permute-start(bf16[320,1280]{1,0:T(8,128)(2,1)S(1)} %get-tuple-element.523), channel_id=1, source_target_pairs={{4,8},{8,4},{5,9},{9,5},{6,10},{10,6},{7,11},{11,7},{20,24},{24,20... | collective-permute-start | bytes 2457608 | tf_op jit(solution)/shard_map/ppermute | solution.py:782
  455.4 51.8 %collective-permute-start.90 = (bf16[128,1280]{1,0:T(8,128)(2,1)S(1)}, bf16[128,1280]{1,0:T(8,128)(2,1)S(1)}, u32[]{:S(2)}, u32[]{:S(2)}) collective-permute-start(bf16[128,1280]{1,0:T(8,128)(2,1)S(1)} %copy-done.101), channel_id=1, source_target_pairs={{0,1},{1,0},{2,3},{3,2},{4,5},{5,4},{6,7},{7,6},{8,9},{9,8},{10,11... | collective-permute-start | bytes 983048 | tf_op jit(solution)/shard_map/ppermute | solution.py:617
  464.5 47.1 %collective-permute-start.86 = (bf16[128,1280]{1,0:T(8,128)(2,1)S(1)}, bf16[128,1280]{1,0:T(8,128)(2,1)S(1)}, u32[]{:S(2)}, u32[]{:S(2)}) collective-permute-start(bf16[128,1280]{1,0:T(8,128)(2,1)S(1)} %add_convert_fusion.23), channel_id=1, source_target_pairs={{0,2},{1,3},{2,0},{3,1},{4,6},{5,7},{6,4},{7,5},{8,10},{9,11},{10,... | collective-permute-start | bytes 983048 | tf_op jit(solution)/shard_map/ppermute | solution.py:620
  521.1 45.4 %collective-permute-start.67 = (bf16[128,1280]{1,0:T(8,128)(2,1)}, bf16[128,1280]{1,0:T(8,128)(2,1)S(1)}, u32[]{:S(2)}, u32[]{:S(2)}) collective-permute-start(bf16[128,1280]{1,0:T(8,128)(2,1)} %get-tuple-element.420), channel_id=1, source_target_pairs={{0,1},{1,0},{2,3},{3,2},{4,5},{5,4},{6,7},{7,6},{8,9},{9,8},{10,11... | collective-permute-start | bytes 983048 | tf_op jit(solution)/shard_map/ppermute | solution.py:617
  521.7 46.2 %collective-permute-start.73 = (bf16[128,1280]{1,0:T(8,128)(2,1)}, bf16[128,1280]{1,0:T(8,128)(2,1)S(1)}, u32[]{:S(2)}, u32[]{:S(2)}) collective-permute-start(bf16[128,1280]{1,0:T(8,128)(2,1)} %get-tuple-element.428), channel_id=1, source_target_pairs={{0,1},{1,0},{2,3},{3,2},{4,5},{5,4},{6,7},{7,6},{8,9},{9,8},{10,11... | collective-permute-start | bytes 983048 | tf_op jit(solution)/shard_map/ppermute | solution.py:617
  528.5 40.7 %collective-permute-start.69 = (bf16[128,1280]{1,0:T(8,128)(2,1)S(1)}, bf16[128,1280]{1,0:T(8,128)(2,1)S(1)}, u32[]{:S(2)}, u32[]{:S(2)}) collective-permute-start(bf16[128,1280]{1,0:T(8,128)(2,1)S(1)} %copy-done.58), channel_id=1, source_target_pairs={{0,2},{1,3},{2,0},{3,1},{4,6},{5,7},{6,4},{7,5},{8,10},{9,11},{10,... | collective-permute-start | bytes 983048 | tf_op jit(solution)/shard_map/ppermute | solution.py:620
  530.0 40.5 %collective-permute-start.75 = (bf16[128,1280]{1,0:T(8,128)(2,1)S(1)}, bf16[128,1280]{1,0:T(8,128)(2,1)S(1)}, u32[]{:S(2)}, u32[]{:S(2)}) collective-permute-start(bf16[128,1280]{1,0:T(8,128)(2,1)S(1)} %add_convert_fusion.25), channel_id=1, source_target_pairs={{0,2},{1,3},{2,0},{3,1},{4,6},{5,7},{6,4},{7,5},{8,10},{9,11},{10,... | collective-permute-start | bytes 983048 | tf_op jit(solution)/shard_map/ppermute | solution.py:620
  531.4 32.5 %collective-permute-start.100 = (f32[8,1280]{1,0:T(8,128)S(1)}, f32[8,1280]{1,0:T(8,128)S(1)}, u32[]{:S(2)}, u32[]{:S(2)}) collective-permute-start(f32[8,1280]{1,0:T(8,128)S(1)} %add.349), channel_id=1, source_target_pairs={{0,4},{4,0},{8,12},{12,8},{1,5},{5,1},{9,13},{13,9},{2,6},{6,2},{1... | collective-permute-start | bytes 122888 | tf_op jit(solution)/shard_map/ppermute | solution.py:623
  563.9 23.0 %collective-permute-start.111 = (bf16[320,1280]{1,0:T(8,128)(2,1)S(1)}, bf16[320,1280]{1,0:T(8,128)(2,1)S(1)}, u32[]{:S(2)}, u32[]{:S(2)}) collective-permute-start(bf16[320,1280]{1,0:T(8,128)(2,1)S(1)} %add_convert_fusion.5), channel_id=1, source_target_pairs={{4,0},{8,12},{5,1},{9,13},{6,2},{10,14},{7,3},{11,15},{20,16},{24,... | collective-permute-start | bytes 2457608 | tf_op jit(solution)/shard_map/ppermute | solution.py:782
  566.5 38.0 %collective-permute-start.112 = (bf16[320,1280]{1,0:T(8,128)(2,1)S(1)}, bf16[320,1280]{1,0:T(8,128)(2,1)S(1)}, u32[]{:S(2)}, u32[]{:S(2)}) collective-permute-start(bf16[320,1280]{1,0:T(8,128)(2,1)S(1)} %add_convert_fusion.4), channel_id=1, source_target_pairs={{4,0},{8,12},{5,1},{9,13},{6,2},{10,14},{7,3},{11,15},{20,16},{24,... | collective-permute-start | bytes 2457608 | tf_op jit(solution)/shard_map/ppermute | solution.py:782
  567.9 82.3 %collective-permute-start.109 = (bf16[320,1280]{1,0:T(8,128)(2,1)}, bf16[320,1280]{1,0:T(8,128)(2,1)}, u32[]{:S(2)}, u32[]{:S(2)}) collective-permute-start(bf16[320,1280]{1,0:T(8,128)(2,1)} %add_convert_fusion.3), channel_id=1, source_target_pairs={{4,0},{8,12},{5,1},{9,13},{6,2},{10,14},{7,3},{11,15},{20,16},{24,... | collective-permute-start | bytes 2457608 | tf_op jit(solution)/shard_map/ppermute | solution.py:782
  569.2 60.6 %collective-permute-start.108 = (bf16[640,320]{0,1:T(8,128)(2,1)S(1)}, bf16[640,320]{0,1:T(8,128)(2,1)S(1)}, u32[]{:S(2)}, u32[]{:S(2)}) collective-permute-start(bf16[640,320]{0,1:T(8,128)(2,1)S(1)} %add_convert_fusion.13), channel_id=1, source_target_pairs={{4,0},{8,12},{5,1},{9,13},{6,2},{10,14},{7,3},{11,15},{20,16},{24,... | collective-permute-start | bytes 1228808 | tf_op jit(solution)/shard_map/ppermute | solution.py:782
  570.5 37.3 %collective-permute-start.102 = (bf16[640,320]{0,1:T(8,128)(2,1)S(1)}, bf16[640,320]{0,1:T(8,128)(2,1)S(1)}, u32[]{:S(2)}, u32[]{:S(2)}) collective-permute-start(bf16[640,320]{0,1:T(8,128)(2,1)S(1)} %copy-done.23), channel_id=1, source_target_pairs={{4,8},{8,4},{5,9},{9,5},{6,10},{10,6},{7,11},{11,7},{20,24},{24,20... | collective-permute-start | bytes 1228808 | tf_op jit(solution)/shard_map/ppermute | solution.py:782
  604.5 30.2 %collective-permute-start.106 = (bf16[640,320]{0,1:T(8,128)(2,1)S(1)}, bf16[640,320]{0,1:T(8,128)(2,1)S(1)}, u32[]{:S(2)}, u32[]{:S(2)}) collective-permute-start(bf16[640,320]{0,1:T(8,128)(2,1)S(1)} %add_convert_fusion.12), channel_id=1, source_target_pairs={{4,0},{8,12},{5,1},{9,13},{6,2},{10,14},{7,3},{11,15},{20,16},{24,... | collective-permute-start | bytes 1228808 | tf_op jit(solution)/shard_map/ppermute | solution.py:782
  607.8 27.8 %collective-permute-start.93 = (bf16[128,1280]{1,0:T(8,128)(2,1)S(1)}, bf16[128,1280]{1,0:T(8,128)(2,1)}, u32[]{:S(2)}, u32[]{:S(2)}) collective-permute-start(bf16[128,1280]{1,0:T(8,128)(2,1)S(1)} %copy-done.60), channel_id=1, source_target_pairs={{0,2},{1,3},{2,0},{3,1},{4,6},{5,7},{6,4},{7,5},{8,10},{9,11},{10,... | collective-permute-start | bytes 983048 | tf_op jit(solution)/shard_map/ppermute | solution.py:620
  609.4 30.9 %collective-permute-start.94 = (bf16[128,1280]{1,0:T(8,128)(2,1)S(1)}, bf16[128,1280]{1,0:T(8,128)(2,1)}, u32[]{:S(2)}, u32[]{:S(2)}) collective-permute-start(bf16[128,1280]{1,0:T(8,128)(2,1)S(1)} %copy-done.60), channel_id=1, source_target_pairs={{0,1},{1,0},{2,3},{3,2},{4,5},{5,4},{6,7},{7,6},{8,9},{9,8},{10,11... | collective-permute-start | bytes 983048 | tf_op jit(solution)/shard_map/ppermute | solution.py:617
  640.3 34.1 %collective-permute-start.110 = (bf16[320,1280]{1,0:T(8,128)(2,1)S(1)}, bf16[320,1280]{1,0:T(8,128)(2,1)S(1)}, u32[]{:S(2)}, u32[]{:S(2)}) collective-permute-start(bf16[320,1280]{1,0:T(8,128)(2,1)S(1)} %add_convert_fusion.2), channel_id=1, source_target_pairs={{4,0},{8,12},{5,1},{9,13},{6,2},{10,14},{7,3},{11,15},{20,16},{24,... | collective-permute-start | bytes 2457608 | tf_op jit(solution)/shard_map/ppermute | solution.py:782
  642.3 30.3 %collective-permute-start.70 = (bf16[128,1280]{1,0:T(8,128)(2,1)S(1)}, bf16[128,1280]{1,0:T(8,128)(2,1)S(1)}, u32[]{:S(2)}, u32[]{:S(2)}) collective-permute-start(bf16[128,1280]{1,0:T(8,128)(2,1)S(1)} %copy-done.34), channel_id=1, source_target_pairs={{0,2},{1,3},{2,0},{3,1},{4,6},{5,7},{6,4},{7,5},{8,10},{9,11},{10,... | collective-permute-start | bytes 983048 | tf_op jit(solution)/shard_map/ppermute | solution.py:620
  643.7 45.5 %collective-permute-start.71 = (bf16[128,1280]{1,0:T(8,128)(2,1)S(1)}, bf16[128,1280]{1,0:T(8,128)(2,1)}, u32[]{:S(2)}, u32[]{:S(2)}) collective-permute-start(bf16[128,1280]{1,0:T(8,128)(2,1)S(1)} %copy-done.34), channel_id=1, source_target_pairs={{0,1},{1,0},{2,3},{3,2},{4,5},{5,4},{6,7},{7,6},{8,9},{9,8},{10,11... | collective-permute-start | bytes 983048 | tf_op jit(solution)/shard_map/ppermute | solution.py:617
  643.9 29.9 %collective-permute-start.76 = (bf16[128,1280]{1,0:T(8,128)(2,1)S(1)}, bf16[128,1280]{1,0:T(8,128)(2,1)}, u32[]{:S(2)}, u32[]{:S(2)}) collective-permute-start(bf16[128,1280]{1,0:T(8,128)(2,1)S(1)} %copy-done.33), channel_id=1, source_target_pairs={{0,2},{1,3},{2,0},{3,1},{4,6},{5,7},{6,4},{7,5},{8,10},{9,11},{10,... | collective-permute-start | bytes 983048 | tf_op jit(solution)/shard_map/ppermute | solution.py:620
  (171 other events, 1813.7 us)
